TPU v7x, 32 devices: a whole 2x2x4 slice. The times are simulated.
32 devices in a mesh: section: 2 (over core), ctx: 4 (over y, x), tp: 4 (over z).
Axes of the slice: x: 2, y: 2, z: 4, core: 2. Of those that a mesh axis runs over, the one named last changes fastest.
Arguments:
- inputs: bfloat16 [4, 1024, 2048], P(None, ('ctx', 'tp')), may hold values from -6 to 6
- segments: int32 [4, 1024], replicated, may hold values from 0 to 3, never falling along the last dimension, each value on 1 to 512 neighbouring positions
- cotangent: bfloat16 [4, 1024, 2048], P(None, ('ctx', 'tp')), may hold values from -6 to 6
- ln_gain: bfloat16 [2, 2048], P('section'), may hold values from 0.5 to 1.5
- ln_bias: bfloat16 [2, 2048], P('section'), may hold values from -3 to 3
- qkv_weight: bfloat16 [2, 3, 2048, 2048], P('section', None, None, 'tp'), may hold values from -1 to 1, as said below
- qkv_bias: bfloat16 [2, 3, 2048], P('section', None, 'tp'), may hold values from -3 to 3
- dense_weight: bfloat16 [2, 2048, 2048], P('section', 'tp'), may hold values from -0.75 to 0.75
- fc1_weight: bfloat16 [2, 2048, 8192], P('section', None, 'tp'), may hold values from -0.125 to 0.125
- fc1_bias: bfloat16 [2, 8192], P('section', 'tp'), may hold values from -3 to 3
- fc2_weight: bfloat16 [2, 8192, 2048], P('section', 'tp'), may hold values from -0.0625 to 0.0625
- out_bias: bfloat16 [2, 2048], P('section'), may hold values from -3 to 3
Outputs:
- layer_outputs: bfloat16 [2, 4, 1024, 2048], P('section', None, ('ctx', 'tp'))
- input_grads: bfloat16 [2, 4, 1024, 2048], P('section', None, ('ctx', 'tp'))
- ln_gain_grad: float32 [2, 2048], P('section')
- ln_bias_grad: float32 [2, 2048], P('section')
- qkv_weight_grad: float32 [2, 3, 2048, 2048], P('section', None, None, 'tp')
- qkv_bias_grad: float32 [2, 3, 2048], P('section', None, 'tp')
- dense_weight_grad: float32 [2, 2048, 2048], P('section', 'tp')
- fc1_weight_grad: float32 [2, 2048, 8192], P('section', None, 'tp')
- fc1_bias_grad: float32 [2, 8192], P('section', 'tp')
- fc2_weight_grad: float32 [2, 8192, 2048], P('section', 'tp')
- out_bias_grad: float32 [2, 2048], P('section')
Inputs may be any that keep to these rules, and one draw needn't show every extreme that they name: `segments`: within a sequence the ids never fall; each of the 4 documents has 1 to 512 tokens, one exactly 512. `qkv_weight`: entries of order 2048^(-1/2).
All inputs are finite; a program needn't handle non-finite values.
Results may differ from a plain program's by a relative error of at most 0.02.
Values may be sent and summed in bfloat16 or wider, within the bound.
No kernel may reach another device: no remote copies, remote signals or barrier semaphores. Data moves between devices by JAX's collectives and lax.ppermute only.
A program may use at most 640 MiB of HBM per device.

v0:
```python
import jax
import jax.numpy as jnp
from jax import lax
from jax.sharding import PartitionSpec as P

HEAD = 64
ROT = 32


EPSILON = 1e-05
NEGATIVE = -1e30
GELU_ROOT = 0.7978845608028654
GELU_CUBE = 0.044715


def from_behind(x, axis, by):
    length = lax.axis_size(axis)
    pairs = [(i, i + by) for i in range(length) if 0 <= i + by < length]
    return lax.ppermute(x, axis, pairs)


def rope_tables(positions, rot_dims):
    half_dims = rot_dims // 2
    frequency = 10000.0 ** (-(2.0 * jnp.arange(half_dims, dtype=jnp.float32)) / rot_dims)
    angles = positions.astype(jnp.float32)[:, None] * frequency[None, :]
    return (jnp.cos(angles)[:, None, :], jnp.sin(angles)[:, None, :])


def rotate(values_in, cosine, sine, rot_dims):
    half_dims = rot_dims // 2
    lower_half = values_in[..., :half_dims]
    upper_half = values_in[..., half_dims:rot_dims]
    return jnp.concatenate(
        [
            lower_half * cosine - upper_half * sine,
            upper_half * cosine + lower_half * sine,
            values_in[..., rot_dims:],
        ],
        axis=-1,
    )


def unrotate(grads_in, cosine, sine, rot_dims):
    half_dims = rot_dims // 2
    lower_half = grads_in[..., :half_dims]
    upper_half = grads_in[..., half_dims:rot_dims]
    return jnp.concatenate(
        [
            lower_half * cosine + upper_half * sine,
            upper_half * cosine - lower_half * sine,
            grads_in[..., rot_dims:],
        ],
        axis=-1,
    )


def gelu_slope(pre_act):
    tangent = jnp.tanh(GELU_ROOT * (pre_act + GELU_CUBE * pre_act * pre_act * pre_act))
    return 0.5 * (1.0 + tangent) + 0.5 * pre_act * (1.0 - tangent * tangent) * GELU_ROOT * (
        1.0 + 3.0 * GELU_CUBE * pre_act * pre_act
    )


def normalize(x_rows):
    centered = x_rows - jnp.mean(x_rows, axis=1, keepdims=True)
    inv_std = lax.rsqrt(jnp.mean(centered * centered, axis=1, keepdims=True) + EPSILON)
    return (centered * inv_std, inv_std)


def take_slot(buffer, slot_index):
    return lax.dynamic_index_in_dim(buffer, slot_index, 0, keepdims=False)


def put_slot(buffer, slot_index, leaf_value, active):
    return lax.dynamic_update_index_in_dim(
        buffer, jnp.where(active, leaf_value, take_slot(buffer, slot_index)), slot_index, 0
    )


def on_device(
    inputs,
    segments,
    cotangent,
    ln_gain,
    ln_bias,
    qkv_weight,
    qkv_bias,
    dense_weight,
    fc1_weight,
    fc1_bias,
    fc2_weight,
    out_bias,
):
    sections = lax.axis_size("section")
    section_id = lax.axis_index("section")
    ctx_id = lax.axis_index("ctx")
    batches, row_count, model_width = inputs.shape
    ctx_rows = row_count * lax.axis_size("tp")
    total_rows = ctx_rows * lax.axis_size("ctx")
    local_dim = qkv_weight.shape[3]
    heads_local = local_dim // HEAD
    score_scale = HEAD ** (-0.5)
    gain_vec = ln_gain[0].astype(jnp.float32)
    shift_vec = ln_bias[0].astype(jnp.float32)
    w_in = jnp.concatenate(
        [qkv_weight[0, 0], qkv_weight[0, 1], qkv_weight[0, 2], fc1_weight[0]], axis=1
    )
    bias_in = jnp.concatenate([qkv_bias[0].reshape(-1), fc1_bias[0]]).astype(jnp.float32)
    w_out = jnp.concatenate([dense_weight[0], fc2_weight[0]], axis=0)
    bias_vec = out_bias[0].astype(jnp.float32)
    query_pos = ctx_id * ctx_rows + jnp.arange(ctx_rows, dtype=jnp.int32)
    cosine, sine = rope_tables(query_pos, ROT)
    key_pos = jnp.arange(total_rows, dtype=jnp.int32)
    contract_rows = (((0,), (0,)), ((), ()))
    contract_cols = (((1,), (1,)), ((), ()))
    received = jnp.zeros((row_count, model_width), jnp.bfloat16)
    layer_out = jnp.zeros((batches, row_count, model_width), jnp.bfloat16)
    buffers = None
    for clock_tick in range(batches + sections - 1):
        micro_batch = clock_tick - section_id
        active = (micro_batch >= 0) & (micro_batch < batches)
        slot_index = jnp.clip(micro_batch, 0, batches - 1)
        x_rows = jnp.where(section_id == 0, take_slot(inputs, slot_index), received).astype(
            jnp.float32
        )
        doc_all = take_slot(segments, slot_index)
        normalized, inv_std = normalize(x_rows)
        normed_b = (normalized * gain_vec + shift_vec).astype(jnp.bfloat16)
        doc_rows = lax.dynamic_slice_in_dim(doc_all, ctx_id * ctx_rows, ctx_rows)
        stored = {}
        projected = jnp.dot(
            lax.all_gather(normed_b, "tp", axis=0, tiled=True),
            w_in,
            preferred_element_type=jnp.float32,
        )
        projected = projected + bias_in
        query_pre = projected[:, :local_dim].reshape(ctx_rows, heads_local, HEAD)
        key_pre = projected[:, local_dim : 2 * local_dim].reshape(ctx_rows, heads_local, HEAD)
        queries_b = rotate(query_pre, cosine, sine, ROT).astype(jnp.bfloat16)
        keys_b = rotate(key_pre, cosine, sine, ROT).astype(jnp.bfloat16)
        values_b = (
            projected[:, 2 * local_dim : 3 * local_dim]
            .reshape(ctx_rows, heads_local, HEAD)
            .astype(jnp.bfloat16)
        )
        up_pre = projected[:, 3 * local_dim :]
        run_max = jnp.full((heads_local, ctx_rows), NEGATIVE, jnp.float32)
        keys_part = lax.all_gather(keys_b, "ctx", axis=0, tiled=True)
        values_part = lax.all_gather(values_b, "ctx", axis=0, tiled=True)
        part_rows = keys_part.shape[0]
        part_pos = jnp.arange(part_rows, dtype=jnp.int32)
        allowed = (part_pos[None, :] <= query_pos[:, None]) & (
            doc_all[None, :] == doc_rows[:, None]
        )
        scores = (
            jnp.einsum("qhd,khd->hqk", queries_b, keys_part, preferred_element_type=jnp.float32)
            * score_scale
        )
        scores = jnp.where(allowed[None], scores, NEGATIVE)
        new_max = jnp.maximum(run_max, jnp.max(scores, axis=2))
        weights = jnp.where(allowed[None], jnp.exp(scores - new_max[:, :, None]), 0.0)
        run_sum = jnp.sum(weights, axis=2)
        accumulated = jnp.einsum(
            "hqk,khd->hqd",
            weights.astype(jnp.bfloat16),
            values_part,
            preferred_element_type=jnp.float32,
        )
        run_max, run_sum, accumulated = (new_max, run_sum, accumulated)
        attended = jnp.transpose(accumulated / run_sum[:, :, None], (1, 0, 2))
        log_total = run_max + jnp.log(run_sum)
        attended_b = attended.reshape(ctx_rows, local_dim).astype(jnp.bfloat16)
        gelu_b = jax.nn.gelu(up_pre, approximate=True).astype(jnp.bfloat16)
        branch_in = jnp.concatenate([attended_b, gelu_b], axis=1)
        branch = lax.psum_scatter(
            jnp.dot(branch_in, w_out, preferred_element_type=jnp.float32).astype(jnp.bfloat16),
            "tp",
            scatter_dimension=0,
            tiled=True,
        ).astype(jnp.float32)
        result = x_rows + branch + bias_vec
        stored["x_rows"] = x_rows.astype(jnp.bfloat16)
        stored["queries"] = queries_b
        stored["keys"] = keys_b
        stored["values"] = values_b
        stored["up_pre"] = up_pre
        stored["branch_in"] = branch_in
        stored["attended"] = attended
        stored["log_total"] = log_total
        result, stored = (result, stored)
        result_b = result.astype(jnp.bfloat16)
        if buffers is None:
            buffers = jax.tree.map(
                lambda leaf_value: jnp.zeros((batches,) + leaf_value.shape, leaf_value.dtype),
                stored,
            )
        buffers = jax.tree.map(
            lambda buffer, leaf_value: put_slot(buffer, slot_index, leaf_value, active),
            buffers,
            stored,
        )
        layer_out = put_slot(layer_out, slot_index, result_b, active)
        received = from_behind(result_b, "section", 1)
    received = jnp.zeros((row_count, model_width), jnp.bfloat16)
    grad_inputs = jnp.zeros((batches, row_count, model_width), jnp.bfloat16)
    totals = None
    for clock_tick in range(batches + sections - 1):
        micro_batch = clock_tick - (sections - 1 - section_id)
        active = (micro_batch >= 0) & (micro_batch < batches)
        slot_index = jnp.clip(micro_batch, 0, batches - 1)
        grad_out = jnp.where(
            section_id == sections - 1, take_slot(cotangent, slot_index), received
        ).astype(jnp.float32)
        stored = jax.tree.map(lambda buffer: take_slot(buffer, slot_index), buffers)
        doc_all = take_slot(segments, slot_index)
        backward_normalized, backward_inv_std = normalize(stored["x_rows"].astype(jnp.float32))
        backward_normed_b = (backward_normalized * gain_vec + shift_vec).astype(jnp.bfloat16)
        backward_doc_rows = lax.dynamic_slice_in_dim(doc_all, ctx_id * ctx_rows, ctx_rows)
        backward_branch_in = stored["branch_in"]
        grad_out_b = grad_out.astype(jnp.bfloat16)
        fold_pieces = lax.all_gather(grad_out_b, "tp", axis=0, tiled=True)
        grad_w = lax.dot_general(
            backward_branch_in, fold_pieces, contract_rows, preferred_element_type=jnp.float32
        )
        grad_rows = lax.dot_general(
            fold_pieces, w_out, contract_cols, preferred_element_type=jnp.float32
        )
        grad_attn_b = (
            grad_rows[:, :local_dim].astype(jnp.bfloat16).reshape(ctx_rows, heads_local, HEAD)
        )
        grad_up = grad_rows[:, local_dim:] * gelu_slope(stored["up_pre"])
        row_delta = jnp.transpose(
            jnp.sum(grad_attn_b.astype(jnp.float32) * stored["attended"], axis=2)
        )
        keys_all = lax.all_gather(stored["keys"], "ctx", axis=0, tiled=True)
        values_all = lax.all_gather(stored["values"], "ctx", axis=0, tiled=True)
        backward_queries_b = stored["queries"]
        backward_allowed = (key_pos[None, :] <= query_pos[:, None]) & (
            doc_all[None, :] == backward_doc_rows[:, None]
        )
        backward_scores = (
            jnp.einsum(
                "qhd,khd->hqk", backward_queries_b, keys_all, preferred_element_type=jnp.float32
            )
            * score_scale
        )
        probs = jnp.where(
            backward_allowed[None], jnp.exp(backward_scores - stored["log_total"][:, :, None]), 0.0
        )
        grad_probs = jnp.einsum(
            "qhd,khd->hqk", grad_attn_b, values_all, preferred_element_type=jnp.float32
        )
        grad_scores_b = (probs * (grad_probs - row_delta[:, :, None])).astype(jnp.bfloat16)
        grad_query = (
            jnp.einsum("hqk,khd->qhd", grad_scores_b, keys_all, preferred_element_type=jnp.float32)
            * score_scale
        )
        probs_b = probs.astype(jnp.bfloat16)
        grad_key_part = (
            jnp.einsum(
                "hqk,qhd->khd",
                grad_scores_b,
                backward_queries_b,
                preferred_element_type=jnp.float32,
            )
            * score_scale
        )
        grad_value_part = jnp.einsum(
            "hqk,qhd->khd", probs_b, grad_attn_b, preferred_element_type=jnp.float32
        )
        key_grads = (
            lax.psum_scatter(
                jnp.concatenate([grad_key_part, grad_value_part], axis=2)
                .reshape(ctx_rows * lax.axis_size("ctx"), 2 * local_dim)
                .astype(jnp.bfloat16),
                "ctx",
                scatter_dimension=0,
                tiled=True,
            )
            .astype(jnp.float32)
            .reshape(ctx_rows, heads_local, 2 * HEAD)
        )
        grad_key_raw = key_grads[..., :HEAD]
        grad_value = key_grads[..., HEAD:]
        grad_key = unrotate(grad_key_raw, cosine, sine, ROT)
        grad_query = unrotate(grad_query, cosine, sine, ROT)
        grad_proj_b = jnp.concatenate(
            [
                grad_query.reshape(ctx_rows, local_dim),
                grad_key.reshape(ctx_rows, local_dim),
                grad_value.reshape(ctx_rows, local_dim),
                grad_up,
            ],
            axis=1,
        ).astype(jnp.bfloat16)
        grad_bias_in = jnp.sum(grad_proj_b.astype(jnp.float32), axis=0)
        grad_w_in = lax.dot_general(
            lax.all_gather(backward_normed_b, "tp", axis=0, tiled=True),
            grad_proj_b,
            contract_rows,
            preferred_element_type=jnp.float32,
        )
        grad_normed = lax.psum_scatter(
            lax.dot_general(
                grad_proj_b, w_in, contract_cols, preferred_element_type=jnp.float32
            ).astype(jnp.bfloat16),
            "tp",
            scatter_dimension=0,
            tiled=True,
        ).astype(jnp.float32)
        grad_gain = jnp.sum(grad_normed * backward_normalized, axis=0)
        grad_shift = jnp.sum(grad_normed, axis=0)
        scaled = grad_normed * gain_vec
        grad_x = grad_out + backward_inv_std * (
            scaled
            - jnp.mean(scaled, axis=1, keepdims=True)
            - backward_normalized * jnp.mean(scaled * backward_normalized, axis=1, keepdims=True)
        )
        grad_x, terms = (
            grad_x,
            (grad_w_in, grad_w, grad_bias_in, grad_gain, grad_shift, jnp.sum(grad_out, axis=0)),
        )
        terms = tuple((jnp.where(active, term_value, 0.0) for term_value in terms))
        totals = terms if totals is None else jax.tree.map(jnp.add, totals, terms)
        grad_x_b = grad_x.astype(jnp.bfloat16)
        grad_inputs = put_slot(grad_inputs, slot_index, grad_x_b, active)
        received = from_behind(grad_x_b, "section", -1)
    total_w_in, total_w_out, total_bias_in, total_gain, total_shift, total_bias_out = totals
    sum_w_in, sum_w_out, sum_bias_in, sum_gain, sum_shift, sum_bias_out = (
        lax.psum(total_w_in.astype(jnp.bfloat16), "ctx").astype(jnp.float32),
        lax.psum(total_w_out.astype(jnp.bfloat16), "ctx").astype(jnp.float32),
        lax.psum(total_bias_in.astype(jnp.bfloat16), "ctx").astype(jnp.float32),
        lax.psum(total_gain.astype(jnp.bfloat16), "ctx").astype(jnp.float32),
        lax.psum(total_shift.astype(jnp.bfloat16), "ctx").astype(jnp.float32),
        lax.psum(total_bias_out.astype(jnp.bfloat16), "ctx").astype(jnp.float32),
    )
    sum_gain, sum_shift, sum_bias_out = lax.psum((sum_gain, sum_shift, sum_bias_out), "tp")
    qkv_grad = jnp.transpose(
        sum_w_in[:, : 3 * local_dim].reshape(model_width, 3, local_dim), (1, 0, 2)
    )
    return (
        layer_out[None],
        grad_inputs[None],
        sum_gain[None],
        sum_shift[None],
        qkv_grad[None],
        sum_bias_in[: 3 * local_dim].reshape(3, local_dim)[None],
        sum_w_out[:local_dim][None],
        sum_w_in[:, 3 * local_dim :][None],
        sum_bias_in[3 * local_dim :][None],
        sum_w_out[local_dim:][None],
        sum_bias_out[None],
    )


def solution(mesh):
    return jax.shard_map(
        on_device,
        mesh=mesh,
        in_specs=(
            P(None, ("ctx", "tp"), None),
            P(),
            P(None, ("ctx", "tp"), None),
            P("section", None),
            P("section", None),
            P("section", None, None, "tp"),
            P("section", None, "tp"),
            P("section", "tp", None),
            P("section", None, "tp"),
            P("section", "tp"),
            P("section", "tp", None),
            P("section", None),
        ),
        out_specs=(
            P("section", None, ("ctx", "tp"), None),
            P("section", None, ("ctx", "tp"), None),
            P("section", None),
            P("section", None),
            P("section", None, None, "tp"),
            P("section", None, "tp"),
            P("section", "tp", None),
            P("section", None, "tp"),
            P("section", "tp"),
            P("section", "tp", None),
            P("section", None),
        ),
        check_vma=False,
    )
```

profile of v0, /device:TPU:0, one launch (start us, length us, event | category | flops | bytes accessed | tf_op | source)
XLA Modules:
  0.0 2297.9 jit_solution(12967685389564836496)
XLA Ops:
  19.1 12.1 pad_maximum_fusion
  31.2 12.5 all-gather.47.cloned.1.call-done
  61.6 18.9 all-gather.49.cloned.1.call-done
  89.4 19.9 all-gather.51.cloned.1.call-done
  124.1 27.4 %reduce-scatter.16.cloned.1.call-done = bf16[64,2048]{1,0:T(8,128)(2,1)} async-done(((bf16[256,2048]{1,0:T(8,128)(2,1)}), bf16[64,2048]{1,0:T(8,128)(2,1)}) %reduce-scatter.16.cloned.1.call-update) | async-done | bytes 262160 | tf_op jit(solution)/shard_map/reduce_scatter | solution.py:175
  156.8 27.9 %all-gather.53.cloned.1.call-done = bf16[256,2048]{1,0:T(8,128)(2,1)} async-done(((bf16[64,2048]{1,0:T(8,128)(2,1)}), bf16[256,2048]{1,0:T(8,128)(2,1)}) %all-gather.53.cloned.1.call-update) | async-done | bytes 1048592 | tf_op jit(solution)/shard_map/all_gather | solution.py:132
  215.8 13.5 all-gather.55.cloned.1.call-done
  238.3 19.2 all-gather.57.cloned.1.call-done
  275.1 26.7 %reduce-scatter.18.cloned.1.call-done = bf16[64,2048]{1,0:T(8,128)(2,1)} async-done(((bf16[256,2048]{1,0:T(8,128)(2,1)}), bf16[64,2048]{1,0:T(8,128)(2,1)}) %reduce-scatter.18.cloned.1.call-update) | async-done | bytes 262160 | tf_op jit(solution)/shard_map/reduce_scatter | solution.py:175
  308.4 27.5 %all-gather.59.cloned.1.call-done = bf16[256,2048]{1,0:T(8,128)(2,1)} async-done(((bf16[64,2048]{1,0:T(8,128)(2,1)}), bf16[256,2048]{1,0:T(8,128)(2,1)}) %all-gather.59.cloned.1.call-update) | async-done | bytes 1048592 | tf_op jit(solution)/shard_map/all_gather | solution.py:132
  363.1 17.4 all-gather.61.cloned.1.call-done
  389.5 19.2 all-gather.63.cloned.1.call-done
  426.4 26.7 %reduce-scatter.20.cloned.1.call-done = bf16[64,2048]{1,0:T(8,128)(2,1)} async-done(((bf16[256,2048]{1,0:T(8,128)(2,1)}), bf16[64,2048]{1,0:T(8,128)(2,1)}) %reduce-scatter.20.cloned.1.call-update) | async-done | bytes 262160 | tf_op jit(solution)/shard_map/reduce_scatter | solution.py:175
  459.4 27.7 %all-gather.65.cloned.1.call-done = bf16[256,2048]{1,0:T(8,128)(2,1)} async-done(((bf16[64,2048]{1,0:T(8,128)(2,1)}), bf16[256,2048]{1,0:T(8,128)(2,1)}) %all-gather.65.cloned.1.call-update) | async-done | bytes 1048592 | tf_op jit(solution)/shard_map/all_gather | solution.py:132
  516.7 14.9 all-gather.67.cloned.1.call-done
  540.7 19.0 all-gather.69.cloned.1.call-done
  598.7 19.9 reduce-scatter.22.cloned.1.call-done
  732.7 20.9 all-gather.95.cloned.1.call-done
  762.5 19.2 all-gather.99.cloned.1.call-done
  853.4 26.6 %reduce-scatter.28.cloned.1.call-done = bf16[64,2048]{1,0:T(8,128)(2,1)} async-done(((bf16[256,2048]{1,0:T(8,128)(2,1)}), bf16[64,2048]{1,0:T(8,128)(2,1)}) %reduce-scatter.28.cloned.1.call-update) | async-done | bytes 262160 | tf_op jit(solution)/shard_map/reduce_scatter | solution.py:303
  892.2 14.6 all-gather.101.cloned.1.call-done
  912.8 23.4 %all-gather.77.cloned.1.call-done = bf16[256,2048]{1,0:T(8,128)(2,1)} async-done(((bf16[64,2048]{1,0:T(8,128)(2,1)}), bf16[256,2048]{1,0:T(8,128)(2,1)}) %all-gather.77.cloned.1.call-update) | async-done | bytes 1048592 | tf_op jit(solution)/shard_map/all_gather | solution.py:221
  983.4 25.3 %reduce-scatter.30.cloned.1.call-done = bf16[256,1024]{0,1:T(8,128)(2,1)} async-done(((bf16[1024,1024]{0,1:T(8,128)(2,1)}), bf16[256,1024]{0,1:T(8,128)(2,1)}) %reduce-scatter.30.cloned.1.call-update) | async-done | bytes 524304 | tf_op jit(solution)/shard_map/reduce_scatter | solution.py:272
  1036.9 25.0 %reduce-scatter.32.cloned.1.call-done = bf16[64,2048]{1,0:T(8,128)(2,1)} async-done(((bf16[256,2048]{1,0:T(8,128)(2,1)}), bf16[64,2048]{1,0:T(8,128)(2,1)}) %reduce-scatter.32.cloned.1.call-update) | async-done | bytes 262160 | tf_op jit(solution)/shard_map/reduce_scatter | solution.py:303
  1074.5 14.1 all-gather.105.cloned.1.call-done
  1094.5 23.6 %all-gather.79.cloned.1.call-done = bf16[256,2048]{1,0:T(8,128)(2,1)} async-done(((bf16[64,2048]{1,0:T(8,128)(2,1)}), bf16[256,2048]{1,0:T(8,128)(2,1)}) %all-gather.79.cloned.1.call-update) | async-done | bytes 1048592 | tf_op jit(solution)/shard_map/all_gather | solution.py:221
  1165.5 25.4 %reduce-scatter.34.cloned.1.call-done = bf16[256,1024]{0,1:T(8,128)(2,1)} async-done(((bf16[1024,1024]{0,1:T(8,128)(2,1)}), bf16[256,1024]{0,1:T(8,128)(2,1)}) %reduce-scatter.34.cloned.1.call-update) | async-done | bytes 524304 | tf_op jit(solution)/shard_map/reduce_scatter | solution.py:272
  1219.8 25.0 %reduce-scatter.36.cloned.1.call-done = bf16[64,2048]{1,0:T(8,128)(2,1)} async-done(((bf16[256,2048]{1,0:T(8,128)(2,1)}), bf16[64,2048]{1,0:T(8,128)(2,1)}) %reduce-scatter.36.cloned.1.call-update) | async-done | bytes 262160 | tf_op jit(solution)/shard_map/reduce_scatter | solution.py:303
  1255.5 16.1 all-gather.109.cloned.1.call-done
  1277.5 23.4 %all-gather.81.cloned.1.call-done = bf16[256,2048]{1,0:T(8,128)(2,1)} async-done(((bf16[64,2048]{1,0:T(8,128)(2,1)}), bf16[256,2048]{1,0:T(8,128)(2,1)}) %all-gather.81.cloned.1.call-update) | async-done | bytes 1048592 | tf_op jit(solution)/shard_map/all_gather | solution.py:221
  1348.2 25.3 %reduce-scatter.38.cloned.1.call-done = bf16[256,1024]{0,1:T(8,128)(2,1)} async-done(((bf16[1024,1024]{0,1:T(8,128)(2,1)}), bf16[256,1024]{0,1:T(8,128)(2,1)}) %reduce-scatter.38.cloned.1.call-update) | async-done | bytes 524304 | tf_op jit(solution)/shard_map/reduce_scatter | solution.py:272
  1402.5 25.0 %reduce-scatter.40.cloned.1.call-done = bf16[64,2048]{1,0:T(8,128)(2,1)} async-done(((bf16[256,2048]{1,0:T(8,128)(2,1)}), bf16[64,2048]{1,0:T(8,128)(2,1)}) %reduce-scatter.40.cloned.1.call-update) | async-done | bytes 262160 | tf_op jit(solution)/shard_map/reduce_scatter | solution.py:303
  1440.0 14.2 all-gather.113.cloned.1.call-done
  1460.7 23.0 %all-gather.83.cloned.1.call-done = bf16[256,2048]{1,0:T(8,128)(2,1)} async-done(((bf16[64,2048]{1,0:T(8,128)(2,1)}), bf16[256,2048]{1,0:T(8,128)(2,1)}) %all-gather.83.cloned.1.call-update) | async-done | bytes 1048592 | tf_op jit(solution)/shard_map/all_gather | solution.py:221
  1491.9 19.4 all-gather.115.cloned.1.call-done
  1580.3 15.2 fusion.526
  1595.6 13.7 fusion.527
  1619.5 13.6 fusion.525
  1643.4 15.7 fusion.524
  1661.3 26.7 %add_convert_fusion.1 = bf16[2560,2048]{1,0:T(8,128)(2,1)} fusion(f32[2560,2048]{1,0:T(8,128)} %fusion.191, f32[2560,2048]{1,0:T(8,128)} %fusion.193, f32[2560,2048]{1,0:T(8,128)} %fusion.195, f32[2560,2048]{1,0:T(8,128)} %fusion.197, bf16[256,2048]{1,0:T(8,128)(2,1)} %all-gather.83.cloned.1.call-done, pred[]{:T(512)S(6)} %and.120, pred[]{:T(512)S(6)} %and.118, ...), kind=kOutput, calls=%fused_computation.1 | convolution fusion | flops 2736783360 | bytes 96731144 | tf_op jit(solution)/shard_map/dot_general | solution.py:222
  1711.6 35.0 %add_convert_fusion = bf16[2048,3584]{1,0:T(8,128)(2,1)} fusion(f32[2048,3584]{1,0:T(8,128)} %fusion.524, f32[2048,3584]{1,0:T(8,128)} %fusion.525, f32[2048,3584]{1,0:T(8,128)} %fusion.526, f32[2048,3584]{1,0:T(8,128)} %fusion.527, bf16[256,2048]{1,0:T(8,128)(2,1)} %all-gather.93.cloned.1.call-done, pred[]{:T(512)S(6)} %and.120, pred[]{:T(512)S(6)} %and.118, ...), kind=kOutput, calls=%fused_computation | convolution fusion | flops 3838836736 | bytes 135004160 | tf_op jit(solution)/shard_map/dot_general | solution.py:297
  1758.1 16.3 all-reduce.1
  1775.6 19.7 all-reduce
  1796.8 407.9 %all-reduce.5.cloned.1.call-done = (bf16[2048,3584]{1,0:T(8,128)(2,1)}, bf16[2560,2048]{1,0:T(8,128)(2,1)}) async-done(((bf16[2048,3584]{1,0:T(8,128)(2,1)}, bf16[2560,2048]{1,0:T(8,128)(2,1)}), (bf16[2048,3584]{1,0:T(8,128)(2,1)}, bf16[2560,2048]{1,0:T(8,128)(2,1)})) %all-reduce.5.cloned.1.call-update) | async-done | bytes 25165840 | tf_op jit(solution)/shard_map/psum | solution.py:330
  2226.1 13.8 convert_element_type.735
  2244.5 12.6 copy.144
  2257.1 12.6 copy.150
  2269.7 21.2 slice_bitcast_fusion
  (889 shorter events, 916.4 us)
Async XLA Ops:
  12.8 67.7 %all-gather.49.cloned.1.call-start = ((), (), s32[]{:S(2)}) async-start(), calls=%async_computation.16 | async-start | bytes 1310720 | tf_op jit(solution)/shard_map/all_gather | solution.py:148
  54.6 54.7 %all-gather.51.cloned.1.call-start = ((), (), s32[]{:S(2)}) async-start(), calls=%async_computation.17 | async-start | bytes 1310720 | tf_op jit(solution)/shard_map/all_gather | solution.py:149
  59.1 92.4 %reduce-scatter.16.cloned.1.call-start = ((), (), s32[]{:S(2)}) async-start(), calls=%async_computation.18 | async-start | bytes 1310720 | tf_op jit(solution)/shard_map/reduce_scatter | solution.py:175
  124.0 60.7 %all-gather.53.cloned.1.call-start = ((), (), s32[]{:S(2)}) async-start(), calls=%async_computation.19 | async-start | bytes 1310720 | tf_op jit(solution)/shard_map/all_gather | solution.py:132
  156.7 72.6 %all-gather.55.cloned.1.call-start = ((), (), s32[]{:S(2)}) async-start(), calls=%async_computation.20 | async-start | bytes 1310720 | tf_op jit(solution)/shard_map/all_gather | solution.py:148
  203.4 54.1 %all-gather.57.cloned.1.call-start = ((), (), s32[]{:S(2)}) async-start(), calls=%async_computation.21 | async-start | bytes 1310720 | tf_op jit(solution)/shard_map/all_gather | solution.py:149
  210.9 90.9 %reduce-scatter.18.cloned.1.call-start = ((), (), s32[]{:S(2)}) async-start(), calls=%async_computation.22 | async-start | bytes 1310720 | tf_op jit(solution)/shard_map/reduce_scatter | solution.py:175
  274.4 61.5 %all-gather.59.cloned.1.call-start = ((), (), s32[]{:S(2)}) async-start(), calls=%async_computation.23 | async-start | bytes 1310720 | tf_op jit(solution)/shard_map/all_gather | solution.py:132
  307.9 72.6 %all-gather.61.cloned.1.call-start = ((), (), s32[]{:S(2)}) async-start(), calls=%async_computation.24 | async-start | bytes 1310720 | tf_op jit(solution)/shard_map/all_gather | solution.py:148
  354.6 54.2 %all-gather.63.cloned.1.call-start = ((), (), s32[]{:S(2)}) async-start(), calls=%async_computation.25 | async-start | bytes 1310720 | tf_op jit(solution)/shard_map/all_gather | solution.py:149
  358.2 94.8 %reduce-scatter.20.cloned.1.call-start = ((), (), s32[]{:S(2)}) async-start(), calls=%async_computation.26 | async-start | bytes 1310720 | tf_op jit(solution)/shard_map/reduce_scatter | solution.py:175
  425.6 61.5 %all-gather.65.cloned.1.call-start = ((), (), s32[]{:S(2)}) async-start(), calls=%async_computation.27 | async-start | bytes 1310720 | tf_op jit(solution)/shard_map/all_gather | solution.py:132
  459.1 72.5 %all-gather.67.cloned.1.call-start = ((), (), s32[]{:S(2)}) async-start(), calls=%async_computation.28 | async-start | bytes 1310720 | tf_op jit(solution)/shard_map/all_gather | solution.py:148
  509.4 79.9 %all-gather.97.cloned.1.call-start = ((), (), s32[]{:S(2)}) async-start(), calls=%async_computation.55 | async-start | bytes 1310720 | tf_op jit(solution)/shard_map/all_gather | solution.py:221
  511.7 106.8 %reduce-scatter.22.cloned.1.call-start = ((), (), s32[]{:S(2)}) async-start(), calls=%async_computation.30 | async-start | bytes 1310720 | tf_op jit(solution)/shard_map/reduce_scatter | solution.py:175
  576.7 75.9 %all-gather.71.cloned.1.call-start = ((), (), s32[]{:S(2)}) async-start(), calls=%async_computation.31 | async-start | bytes 1310720 | tf_op jit(solution)/shard_map/all_gather | solution.py:132
  625.6 85.6 %all-gather.73.cloned.1.call-start = ((), (), s32[]{:S(2)}) async-start(), calls=%async_computation.32 | async-start | bytes 1310720 | tf_op jit(solution)/shard_map/all_gather | solution.py:148
  685.2 68.3 %all-gather.95.cloned.1.call-start = ((), (), s32[]{:S(2)}) async-start(), calls=%async_computation.54 | async-start | bytes 1310720 | tf_op jit(solution)/shard_map/all_gather | solution.py:235
  697.6 84.1 %all-gather.99.cloned.1.call-start = ((), (), s32[]{:S(2)}) async-start(), calls=%async_computation.56 | async-start | bytes 1310720 | tf_op jit(solution)/shard_map/all_gather | solution.py:236
  709.0 117.8 %reduce-scatter.26.cloned.1.call-start = ((), (), s32[]{:S(2)}) async-start(), calls=%async_computation.35 | async-start | bytes 2621440 | tf_op jit(solution)/shard_map/reduce_scatter | solution.py:272
  791.4 88.6 %reduce-scatter.28.cloned.1.call-start = ((), (), s32[]{:S(2)}) async-start(), calls=%async_computation.36 | async-start | bytes 1310720 | tf_op jit(solution)/shard_map/reduce_scatter | solution.py:303
  852.6 54.2 %all-gather.101.cloned.1.call-start = ((), (), s32[]{:S(2)}) async-start(), calls=%async_computation.57 | async-start | bytes 1310720 | tf_op jit(solution)/shard_map/all_gather | solution.py:235
  853.4 82.9 %all-gather.77.cloned.1.call-start = ((), (), s32[]{:S(2)}) async-start(), calls=%async_computation.37 | async-start | bytes 1310720 | tf_op jit(solution)/shard_map/all_gather | solution.py:221
  891.3 72.3 %all-gather.103.cloned.1.call-start = ((), (), s32[]{:S(2)}) async-start(), calls=%async_computation.58 | async-start | bytes 1310720 | tf_op jit(solution)/shard_map/all_gather | solution.py:236
  891.9 116.8 %reduce-scatter.30.cloned.1.call-start = ((), (), s32[]{:S(2)}) async-start(), calls=%async_computation.38 | async-start | bytes 2621440 | tf_op jit(solution)/shard_map/reduce_scatter | solution.py:272
  973.3 88.6 %reduce-scatter.32.cloned.1.call-start = ((), (), s32[]{:S(2)}) async-start(), calls=%async_computation.39 | async-start | bytes 1310720 | tf_op jit(solution)/shard_map/reduce_scatter | solution.py:303
  1034.5 54.0 %all-gather.105.cloned.1.call-start = ((), (), s32[]{:S(2)}) async-start(), calls=%async_computation.59 | async-start | bytes 1310720 | tf_op jit(solution)/shard_map/all_gather | solution.py:235
  1035.1 83.0 %all-gather.79.cloned.1.call-start = ((), (), s32[]{:S(2)}) async-start(), calls=%async_computation.40 | async-start | bytes 1310720 | tf_op jit(solution)/shard_map/all_gather | solution.py:221
  1073.2 72.5 %all-gather.107.cloned.1.call-start = ((), (), s32[]{:S(2)}) async-start(), calls=%async_computation.60 | async-start | bytes 1310720 | tf_op jit(solution)/shard_map/all_gather | solution.py:236
  1074.0 116.9 %reduce-scatter.34.cloned.1.call-start = ((), (), s32[]{:S(2)}) async-start(), calls=%async_computation.41 | async-start | bytes 2621440 | tf_op jit(solution)/shard_map/reduce_scatter | solution.py:272
  1155.5 89.3 %reduce-scatter.36.cloned.1.call-start = ((), (), s32[]{:S(2)}) async-start(), calls=%async_computation.42 | async-start | bytes 1310720 | tf_op jit(solution)/shard_map/reduce_scatter | solution.py:303
  1217.3 54.2 %all-gather.109.cloned.1.call-start = ((), (), s32[]{:S(2)}) async-start(), calls=%async_computation.61 | async-start | bytes 1310720 | tf_op jit(solution)/shard_map/all_gather | solution.py:235
  1218.1 82.9 %all-gather.81.cloned.1.call-start = ((), (), s32[]{:S(2)}) async-start(), calls=%async_computation.43 | async-start | bytes 1310720 | tf_op jit(solution)/shard_map/all_gather | solution.py:221
  1254.6 73.8 %all-gather.111.cloned.1.call-start = ((), (), s32[]{:S(2)}) async-start(), calls=%async_computation.62 | async-start | bytes 1310720 | tf_op jit(solution)/shard_map/all_gather | solution.py:236
  1255.2 118.3 %reduce-scatter.38.cloned.1.call-start = ((), (), s32[]{:S(2)}) async-start(), calls=%async_computation.44 | async-start | bytes 2621440 | tf_op jit(solution)/shard_map/reduce_scatter | solution.py:272
  1338.2 89.3 %reduce-scatter.40.cloned.1.call-start = ((), (), s32[]{:S(2)}) async-start(), calls=%async_computation.45 | async-start | bytes 1310720 | tf_op jit(solution)/shard_map/reduce_scatter | solution.py:303
  1400.0 54.2 %all-gather.113.cloned.1.call-start = ((), (), s32[]{:S(2)}) async-start(), calls=%async_computation.63 | async-start | bytes 1310720 | tf_op jit(solution)/shard_map/all_gather | solution.py:235
  1400.7 83.0 %all-gather.83.cloned.1.call-start = ((), (), s32[]{:S(2)}) async-start(), calls=%async_computation.46 | async-start | bytes 1310720 | tf_op jit(solution)/shard_map/all_gather | solution.py:221
  1437.3 74.1 %all-gather.115.cloned.1.call-start = ((), (), s32[]{:S(2)}) async-start(), calls=%async_computation.64 | async-start | bytes 1310720 | tf_op jit(solution)/shard_map/all_gather | solution.py:236
  1438.0 142.3 %all-gather.87.cloned.1.call-start = ((), (), s32[]{:S(2)}) async-start(), calls=%async_computation.50 | async-start | bytes 1310720 | tf_op jit(solution)/shard_map/all_gather | solution.py:298
  1438.6 156.9 %all-gather.85.cloned.1.call-start = ((), (), s32[]{:S(2)}) async-start(), calls=%async_computation.49 | async-start | bytes 1310720 | tf_op jit(solution)/shard_map/all_gather | solution.py:298
  1439.4 180.1 %all-gather.89.cloned.1.call-start = ((), (), s32[]{:S(2)}) async-start(), calls=%async_computation.51 | async-start | bytes 1310720 | tf_op jit(solution)/shard_map/all_gather | solution.py:298
  1439.9 203.4 %all-gather.91.cloned.1.call-start = ((), (), s32[]{:S(2)}) async-start(), calls=%async_computation.52 | async-start | bytes 1310720 | tf_op jit(solution)/shard_map/all_gather | solution.py:298
  1460.2 231.4 %reduce-scatter.42.cloned.1.call-start = ((), (), s32[]{:S(2)}) async-start(), calls=%async_computation.47 | async-start | bytes 2621440 | tf_op jit(solution)/shard_map/reduce_scatter | solution.py:272
  1526.3 185.2 %all-gather.93.cloned.1.call-start = ((), (), s32[]{:S(2)}) async-start(), calls=%async_computation.53 | async-start | bytes 1310720 | tf_op jit(solution)/shard_map/all_gather | solution.py:298
  1544.1 204.9 %reduce-scatter.24.cloned.1.call-start = ((), (), s32[]{:S(2)}) async-start(), calls=%async_computation.34 | async-start | bytes 1310720 | tf_op jit(solution)/shard_map/reduce_scatter | solution.py:175
  1557.1 199.5 %reduce-scatter.44.cloned.1.call-start = ((), (), s32[]{:S(2)}) async-start(), calls=%async_computation.48 | async-start | bytes 1310720 | tf_op jit(solution)/shard_map/reduce_scatter | solution.py:303
  1711.4 493.3 %all-reduce.5.cloned.1.call-start = ((), (), s32[]{:S(2)}) async-start(), calls=%async_computation.65 | async-start | bytes 50331648 | tf_op jit(solution)/shard_map/psum | solution.py:330
  (193 other events, 8569.0 us)
Sparse Core Ops, SparseCore 0:
  13.0 30.6 all-gather.46
  54.7 25.7 all-gather.48
  82.9 26.3 all-gather.50
  124.1 27.2 reduce-scatter.15
  156.8 27.7 all-gather.52
  203.5 25.7 all-gather.54
  231.1 26.3 all-gather.56
  274.5 27.2 reduce-scatter.17
  308.0 27.7 all-gather.58
  354.7 25.7 all-gather.60
  382.3 26.3 all-gather.62
  425.7 27.2 reduce-scatter.19
  459.3 27.7 all-gather.64
  505.8 25.7 all-gather.66
  533.3 26.3 all-gather.68
  561.1 27.9 all-gather.96
  591.8 26.6 reduce-scatter.21
  625.7 26.8 all-gather.70
  671.4 25.7 all-gather.72
  698.9 26.3 all-gather.74
  727.1 26.3 all-gather.94
  755.3 26.3 all-gather.98
  791.5 35.1 reduce-scatter.25
  852.7 27.2 reduce-scatter.27
  908.2 27.9 all-gather.76
  937.9 25.7 all-gather.102
  973.5 35.1 reduce-scatter.29
  1034.6 27.2 reduce-scatter.31
  1090.1 27.9 all-gather.78
  1120.0 25.7 all-gather.106
  1155.6 35.1 reduce-scatter.33
  1217.5 27.2 reduce-scatter.35
  1246.6 24.8 all-gather.108
  1272.9 27.9 all-gather.80
  1302.6 25.7 all-gather.110
  1338.3 35.1 reduce-scatter.37
  1400.1 27.2 reduce-scatter.39
  1455.8 27.9 all-gather.82
  1485.6 25.7 all-gather.114
  1512.8 27.9 all-gather.86
  1542.4 27.3 all-gather.84
  1571.2 27.3 all-gather.88
  1600.0 27.3 all-gather.90
  1630.2 34.5 reduce-scatter.41
  1666.2 27.9 all-gather.92
  1696.4 26.6 reduce-scatter.23
  1726.0 25.7 reduce-scatter.43
  1756.0 448.7 all-reduce.4
  (3 shorter events, 74.4 us)
where the time goes:
time: 2310 us; the launch traced here: 2300 us
  waiting for transfers between devices  1210 us (52%)
  matrix products  483 us (21%)
  local copies, waits for them, and re-layouts  269 us (12%)
  other arithmetic  261 us (11%)
  blocking collectives  36 us (2%)
    psum x1, waiting for transfers between devices, on_device(): lax.psum(total_w_in.astype(jnp.bfloat16), 'ctx').astype(jnp.float32)  408 us
    all_gather x5, waiting for transfers between devices, on_device(): lax.all_gather(normed_b, 'tp', axis=0, tiled=True)  107 us
    reduce_scatter x5, waiting for transfers between devices, on_device(): lax.psum_scatter(lax.dot_general(grad_proj_b, w_in, contract_cols, prefer...  102 us
    reduce_scatter x5, waiting for transfers between devices, on_device(): lax.psum_scatter(jnp.dot(branch_in, w_out, preferred_element_type=jnp.flo...  101 us
    all_gather x5, waiting for transfers between devices, on_device(): fold_pieces = lax.all_gather(grad_out_b, 'tp', axis=0, tiled=True)  93.5 us
    dot_general x5, matrix products, on_device(): lax.dot_general(lax.all_gather(backward_normed_b, 'tp', axis=0, tiled=Tru...  93.2 us
    reduce_scatter x5, waiting for transfers between devices, on_device(): lax.psum_scatter(jnp.concatenate([grad_key_part, grad_value_part], axis=2...  86.3 us
    all_gather x5, waiting for transfers between devices, on_device(): values_part = lax.all_gather(values_b, 'ctx', axis=0, tiled=True)  85.1 us
  transfers between devices with their start and end apart: 59, of which 48 were waited for; matrix products, arithmetic and copies ran while one was open for 26% of the time, Pallas kernels for 0%

commit v1 on v0

v1 whole, which is shorter than its diff:
```python
import functools

import jax
import jax.numpy as jnp
from jax import lax
from jax.experimental import pallas as pl
from jax.experimental.pallas import tpu as pltpu
from jax.sharding import PartitionSpec as P

HEAD = 64
ROT = 32
PAIR = 2 * HEAD

EPSILON = 1e-05
NEGATIVE = -1e30
GELU_ROOT = 0.7978845608028654
GELU_CUBE = 0.044715

BF = jnp.bfloat16
F32 = jnp.float32
NT = (((1,), (1,)), ((), ()))
TN = (((0,), (0,)), ((), ()))
VMEM_LIMIT = 60 * 1024 * 1024


def sds(shape, dtype):
    return jax.ShapeDtypeStruct(shape, dtype)


def nbytes(*arrays):
    return sum(a.size * a.dtype.itemsize for a in arrays)


def call(kernel, grid, scalars, ins, in_specs, outs, out_specs, flops, name, scratch=(), moved=None):
    return pl.pallas_call(
        kernel,
        grid_spec=pltpu.PrefetchScalarGridSpec(
            num_scalar_prefetch=len(scalars),
            grid=grid,
            in_specs=in_specs,
            out_specs=out_specs,
            scratch_shapes=scratch,
        ),
        out_shape=outs,
        name=name,
        cost_estimate=pl.CostEstimate(
            flops=int(flops),
            bytes_accessed=int(moved if moved is not None else nbytes(*ins) + nbytes(*jax.tree.leaves(outs))),
            transcendentals=0,
        ),
        compiler_params=pltpu.CompilerParams(vmem_limit_bytes=VMEM_LIMIT),
    )(*scalars, *ins)


def dot(a, b, dims=(((1,), (0,)), ((), ()))):
    return lax.dot_general(a, b, dims, preferred_element_type=F32)


def whole(shape):
    return pl.BlockSpec(shape, lambda *_: (0,) * len(shape))


def picked(shape, which, index):
    def index_map(*args):
        ids, sel = args[:-1], args[-1]
        return tuple(jnp.where(sel[0] == which, i, 0) for i in index(*ids))

    return pl.BlockSpec(shape, index_map)


def on_pick(sel, own, other, body):
    @pl.when(sel[0] == 0)
    def _():
        body(*own)

    @pl.when(sel[0] != 0)
    def _():
        body(*other)


def center(x):
    c = x - jnp.mean(x, axis=1, keepdims=True)
    r = lax.rsqrt(jnp.mean(c * c, axis=1, keepdims=True) + EPSILON)
    return c * r, r


def norm_first_kernel(x, gain, shift, o):
    n, _ = center(x[...].astype(F32))
    o[...] = (n * gain[...] + shift[...]).astype(BF)


def norm_first(x, gain, shift):
    return call(
        norm_first_kernel, (1,), (), (x, gain, shift),
        [whole(x.shape), whole(gain.shape), whole(shift.shape)],
        sds(x.shape, BF), whole(x.shape), 10 * x.size, "norm_first",
    )


def norm_next_kernel(x, branch, bias, gain, shift, y, o):
    total = x[...].astype(F32) + branch[...].astype(F32) + bias[...]
    rounded = total.astype(BF)
    y[...] = rounded
    n, _ = center(rounded.astype(F32))
    o[...] = (n * gain[...] + shift[...]).astype(BF)


def norm_next(x, branch, bias, gain, shift):
    v = whole(gain.shape)
    return call(
        norm_next_kernel, (1,), (), (x, branch, bias, gain, shift),
        [whole(x.shape), whole(x.shape), v, v, v],
        (sds(x.shape, BF), sds(x.shape, BF)), (whole(x.shape), whole(x.shape)),
        12 * x.size, "norm_next",
    )


def norm_back_kernel(x, gn, g, gain, gx, sums):
    n, r = center(x[...].astype(F32))
    up = gn[...].astype(F32)
    out = g[...].astype(F32)
    s = up * gain[...]
    gx[...] = (
        out
        + r * (s - jnp.mean(s, axis=1, keepdims=True) - n * jnp.mean(s * n, axis=1, keepdims=True))
    ).astype(BF)
    sums[0:1, :] = jnp.sum(up * n, axis=0, keepdims=True)
    sums[1:2, :] = jnp.sum(up, axis=0, keepdims=True)
    sums[2:3, :] = jnp.sum(out, axis=0, keepdims=True)


def norm_back(x, gn, g, gain):
    w = whole(x.shape)
    return call(
        norm_back_kernel, (1,), (), (x, gn, g, gain),
        [w, w, w, whole(gain.shape)],
        (sds(x.shape, BF), sds((3, x.shape[1]), F32)), (w, whole((3, x.shape[1]))),
        20 * x.size, "norm_back",
    )


def turn(a, cosine, low, high, sign):
    width = a.shape[-1]
    half = ROT // 2
    up = pltpu.roll(a, width - half, 1) * low
    down = pltpu.roll(a, half, 1) * high
    return a * cosine + (down - up if sign > 0 else up - down)


def project_kernel(sel, x, own, other, bias, cosine, low, high, q, kv):
    step = pl.program_id(0)

    def body(w):
        a = dot(x[...], w[0]) + bias[0]

        @pl.when(step == 0)
        def _():
            kv[0] = turn(a, cosine[...], low[...], high[...], 1).astype(BF)

        @pl.when(step == 1)
        def _():
            kv[0] = a.astype(BF)

        @pl.when(step == 2)
        def _():
            q[...] = turn(a, cosine[...], low[...], high[...], 1).astype(BF)

    on_pick(sel, (own,), (other,), body)


def project(sel, x, own, other, bias, tables):
    rows, width = x.shape
    local = own.shape[2]
    blk = min(256, local)
    n = local // blk

    def w_index(c, j):
        return (lax.rem(c + 1, 3), 0, j)

    table = whole((rows, blk))
    return call(
        project_kernel, (3, n), (sel,), (x, own, other, bias, *tables),
        [
            whole(x.shape),
            picked((1, width, blk), 0, w_index),
            picked((1, width, blk), 1, w_index),
            pl.BlockSpec((1, 1, blk), lambda c, j, s: (lax.rem(c + 1, 3), 0, j)),
            table, table, table,
        ],
        (sds((rows, local), BF), sds((2, rows, local), BF)),
        (
            pl.BlockSpec((rows, blk), lambda c, j, s: (0, jnp.where(c == 2, j, 0))),
            pl.BlockSpec(
                (1, rows, blk),
                lambda c, j, s: (jnp.minimum(c, 1), 0, jnp.where(c == 2, n - 1, j)),
            ),
        ),
        6 * rows * width * local, "project", moved=nbytes(own, x) + 6 * rows * local,
    )


def expand_kernel(sel, x, own, other, bias, gelu, slope):
    def body(w):
        u = dot(x[...], w[...]) + bias[...]
        t = jnp.tanh(GELU_ROOT * (u + GELU_CUBE * u * u * u))
        gelu[...] = (0.5 * u * (1.0 + t)).astype(BF)
        slope[...] = (
            0.5 * (1.0 + t)
            + 0.5 * u * (1.0 - t * t) * GELU_ROOT * (1.0 + 3.0 * GELU_CUBE * u * u)
        ).astype(BF)

    on_pick(sel, (own,), (other,), body)


def expand(sel, x, own, other, bias):
    rows, width = x.shape
    hidden = own.shape[1]
    blk = 256
    out = pl.BlockSpec((rows, blk), lambda j, s: (0, j))
    return call(
        expand_kernel, (hidden // blk,), (sel,), (x, own, other, bias),
        [
            whole(x.shape),
            picked((width, blk), 0, lambda j: (0, j)),
            picked((width, blk), 1, lambda j: (0, j)),
            pl.BlockSpec((1, blk), lambda j, s: (0, j)),
        ],
        (sds((rows, hidden), BF), sds((rows, hidden), BF)), (out, out),
        2 * rows * width * hidden, "expand", moved=nbytes(own, x) + 4 * rows * hidden,
    )


def contract_kernel(sel, a, u, d_own, f_own, d_other, f_other, o):
    def body(d, f):
        o[...] = (dot(a[...], d[...]) + dot(u[...], f[...])).astype(BF)

    on_pick(sel, (d_own, f_own), (d_other, f_other), body)


def contract(sel, a, u, d_own, f_own, d_other, f_other):
    rows, local = a.shape
    hidden = u.shape[1]
    width = d_own.shape[1]
    blk = 256
    specs = [
        picked((k, blk), which, lambda j: (0, j)) for which in (0, 1) for k in (local, hidden)
    ]
    return call(
        contract_kernel, (width // blk,), (sel,), (a, u, d_own, f_own, d_other, f_other),
        [whole(a.shape), whole(u.shape)] + specs,
        sds((rows, width), BF), pl.BlockSpec((rows, blk), lambda j, s: (0, j)),
        2 * rows * (local + hidden) * width, "contract",
        moved=nbytes(a, u, d_own, f_own) + 2 * rows * width,
    )


def masks_of(blocks, rows, drow, dcol):
    found = []
    for j in range(blocks):
        same = dcol[j * rows : (j + 1) * rows, :] == drow[...]
        if j == 0:
            key = lax.broadcasted_iota(jnp.int32, (rows, rows), 0)
            query = lax.broadcasted_iota(jnp.int32, (rows, rows), 1)
            same = same & (key <= query)
        found.append(same)
    return found


def attend_kernel(blocks, *refs):
    q, drow, dcol = refs[0], refs[1], refs[2]
    kvs = refs[3 : 3 + blocks]
    o, lse = refs[3 + blocks :]
    rows = q.shape[0]
    first = lax.broadcasted_iota(jnp.int32, (rows, PAIR), 1) < HEAD
    scaled = q[...] * HEAD ** (-0.5)
    allowed = masks_of(blocks, rows, drow, dcol)
    halves = []
    for h in range(2):
        qh = jnp.where(first if h == 0 else ~first, scaled, jnp.zeros_like(scaled))
        scores = [
            jnp.where(allowed[j], dot(kvs[j][0], qh, NT), NEGATIVE) for j in range(blocks)
        ]
        top = functools.reduce(
            jnp.maximum, [jnp.max(s, axis=0, keepdims=True) for s in scores]
        )
        weights = [jnp.exp(s - top) for s in scores]
        total = sum(jnp.sum(w, axis=0, keepdims=True) for w in weights)
        out = sum(dot(kvs[j][1], weights[j].astype(BF), TN) for j in range(blocks))
        halves.append((out / total)[h * HEAD : (h + 1) * HEAD])
        lse[0, h : h + 1, :] = top + jnp.log(total)
    o[...] = jnp.transpose(jnp.concatenate(halves, axis=0)).astype(BF)


def attend(q, kvs, drow, dcol):
    rows, local = q.shape
    blocks = len(kvs)
    pairs = local // PAIR
    return call(
        functools.partial(attend_kernel, blocks), (pairs,), (), (q, drow, dcol, *kvs),
        [
            pl.BlockSpec((rows, PAIR), lambda p: (0, p)),
            whole(drow.shape), whole(dcol.shape),
        ]
        + [pl.BlockSpec((2, rows, PAIR), lambda p: (0, 0, p))] * blocks,
        (sds((rows, local), BF), sds((pairs, 8, rows), F32)),
        (
            pl.BlockSpec((rows, PAIR), lambda p: (0, p)),
            pl.BlockSpec((1, 8, rows), lambda p: (p, 0, 0)),
        ),
        8 * rows * rows * blocks * local, "attend",
    )


def attend_back_kernel(blocks, *refs):
    q, go, lse, drow, dcol, cosine, low, high = refs[:8]
    kvs = refs[8 : 8 + blocks]
    gq = refs[8 + blocks]
    gkvs = refs[9 + blocks :]
    rows = q.shape[0]
    first = lax.broadcasted_iota(jnp.int32, (rows, PAIR), 1) < HEAD
    scaled = q[...] * HEAD ** (-0.5)
    gout = go[...]
    allowed = masks_of(blocks, rows, drow, dcol)
    gk = [0.0] * blocks
    gv = [0.0] * blocks
    halves = []
    for h in range(2):
        mine = first if h == 0 else ~first
        qh = jnp.where(mine, scaled, jnp.zeros_like(scaled))
        gh = jnp.where(mine, gout, jnp.zeros_like(gout))
        shift = lse[0, h : h + 1, :]
        probs = [
            jnp.where(allowed[j], jnp.exp(dot(kvs[j][0], qh, NT) - shift), 0.0)
            for j in range(blocks)
        ]
        gprobs = [dot(kvs[j][1], gh, NT) for j in range(blocks)]
        delta = sum(
            jnp.sum(probs[j] * gprobs[j], axis=0, keepdims=True) for j in range(blocks)
        )
        gqt = 0.0
        for j in range(blocks):
            gs = (probs[j] * (gprobs[j] - delta)).astype(BF)
            gk[j] += dot(gs, qh)
            gv[j] += dot(probs[j].astype(BF), gh)
            gqt += dot(kvs[j][0], gs, TN)
        halves.append(gqt[h * HEAD : (h + 1) * HEAD])
    full = jnp.transpose(jnp.concatenate(halves, axis=0)) * HEAD ** (-0.5)
    gq[...] = turn(full, cosine[...], low[...], high[...], -1).astype(BF)
    for j in range(blocks):
        gkvs[j][0] = gk[j].astype(gkvs[j].dtype)
        gkvs[j][1] = gv[j].astype(gkvs[j].dtype)


def attend_back(q, kvs, go, lse, drow, dcol, tables):
    rows, local = q.shape
    blocks = len(kvs)
    pair = pl.BlockSpec((rows, PAIR), lambda p: (0, p))
    two = pl.BlockSpec((2, rows, PAIR), lambda p: (0, 0, p))
    table = pl.BlockSpec((rows, PAIR), lambda p: (0, 0))
    return call(
        functools.partial(attend_back_kernel, blocks), (local // PAIR,), (),
        (q, go, lse, drow, dcol, *tables, *kvs),
        [
            pair, pair, pl.BlockSpec((1, 8, rows), lambda p: (p, 0, 0)),
            whole(drow.shape), whole(dcol.shape), table, table, table,
        ]
        + [two] * blocks,
        (sds((rows, local), BF),)
        + tuple(sds((2, rows, local), F32 if j == 0 else BF) for j in range(blocks)),
        (pair,) + (two,) * blocks,
        20 * rows * rows * blocks * local, "attend_back",
    )


def join_kernel(count, *refs):
    gq, own = refs[0], refs[1]
    got = refs[2 : 2 + count]
    cosine, low, high, out = refs[2 + count :]
    gk = sum((r[0].astype(F32) for r in got), own[0])
    gv = sum((r[1].astype(F32) for r in got), own[1])
    out[0] = gq[...]
    out[1] = turn(gk, cosine[...], low[...], high[...], -1).astype(BF)
    out[2] = gv.astype(BF)


def join(gq, own, got, tables):
    rows, local = gq.shape
    two = pl.BlockSpec((2, rows, PAIR), lambda p: (0, 0, p))
    table = pl.BlockSpec((rows, PAIR), lambda p: (0, 0))
    return call(
        functools.partial(join_kernel, len(got)), (local // PAIR,), (), (gq, own, *got, *tables),
        [pl.BlockSpec((rows, PAIR), lambda p: (0, p)), two] + [two] * len(got) + [table] * 3,
        sds((3, rows, local), BF), pl.BlockSpec((3, rows, PAIR), lambda p: (0, 0, p)),
        10 * own.size, "join",
    )


def spread_attn_kernel(sel, g, own, other, o):
    def body(w):
        o[...] = dot(g[...], w[...], NT).astype(BF)

    on_pick(sel, (own,), (other,), body)


def spread_attn(sel, g, own, other):
    rows, width = g.shape
    local = own.shape[0]
    blk = min(256, local)
    return call(
        spread_attn_kernel, (local // blk,), (sel,), (g, own, other),
        [
            whole(g.shape),
            picked((blk, width), 0, lambda j: (j, 0)),
            picked((blk, width), 1, lambda j: (j, 0)),
        ],
        sds((rows, local), BF), pl.BlockSpec((rows, blk), lambda j, s: (0, j)),
        2 * rows * width * local, "spread_attn", moved=nbytes(g, own) + 2 * rows * local,
    )


def spread_up_kernel(sel, g, own, other, slope, o, sums):
    def body(w):
        u = (dot(g[...], w[...], NT) * slope[...].astype(F32)).astype(BF)
        o[...] = u
        sums[...] = jnp.sum(u.astype(F32), axis=0, keepdims=True)

    on_pick(sel, (own,), (other,), body)


def spread_up(sel, g, own, other, slope):
    rows, width = g.shape
    hidden = own.shape[0]
    blk = 256
    col = pl.BlockSpec((rows, blk), lambda j, s: (0, j))
    return call(
        spread_up_kernel, (hidden // blk,), (sel,), (g, own, other, slope),
        [
            whole(g.shape),
            picked((blk, width), 0, lambda j: (j, 0)),
            picked((blk, width), 1, lambda j: (j, 0)),
            col,
        ],
        (sds((rows, hidden), BF), sds((1, hidden), F32)),
        (col, pl.BlockSpec((1, blk), lambda j, s: (0, j))),
        2 * rows * width * hidden, "spread_up", moved=nbytes(g, own, slope) + 2 * rows * hidden,
    )


def gather_grad_kernel(sel, qkv, up, w_own, f_own, w_other, f_other, o, sums):
    def body(w, f):
        a = dot(up[...], f[...], NT)
        for c in range(3):
            a += dot(qkv[c], w[c], NT)
        o[...] = a.astype(BF)

    on_pick(sel, (w_own, f_own), (w_other, f_other), body)

    @pl.when(pl.program_id(0) == 0)
    def _():
        for c in range(3):
            sums[c : c + 1, :] = jnp.sum(qkv[c].astype(F32), axis=0, keepdims=True)


def gather_grad(sel, qkv, up, w_own, f_own, w_other, f_other):
    _, rows, local = qkv.shape
    hidden = up.shape[1]
    width = f_own.shape[0]
    blk = 256
    specs = []
    for which in (0, 1):
        specs.append(picked((3, blk, local), which, lambda j: (0, j, 0)))
        specs.append(picked((blk, hidden), which, lambda j: (j, 0)))
    return call(
        gather_grad_kernel, (width // blk,), (sel,), (qkv, up, w_own, f_own, w_other, f_other),
        [whole(qkv.shape), whole(up.shape)] + specs,
        (sds((rows, width), BF), sds((3, local), F32)),
        (pl.BlockSpec((rows, blk), lambda j, s: (0, j)), whole((3, local))),
        2 * rows * width * (3 * local + hidden), "gather_grad",
        moved=nbytes(qkv, up, w_own, f_own) + 2 * rows * width,
    )


def weight_kernel(count, adds, half, *refs):
    lhs, rhs = refs[:count], refs[count : 2 * count]
    a = sum(dot(x[...], y[0], TN) for x, y in zip(lhs, rhs))
    if adds:
        a += refs[2 * count][0].astype(F32)
    refs[-1][0] = a.astype(BF)


def weight_half(half, lhs, rhs, add=None):
    rows, depth = lhs[0].shape
    planes, _, cols = rhs[0].shape
    blk = min(256, depth // 2)
    n = depth // 2 // blk
    ins = (*lhs, *rhs) + (() if add is None else (add,))
    out = pl.BlockSpec((1, blk, cols), lambda c, i, h: (c, i, 0))
    return call(
        functools.partial(weight_kernel, len(lhs), add is not None), (planes, n), (half,), ins,
        [pl.BlockSpec((rows, blk), lambda c, i, h: (0, h[0] * n + i))] * len(lhs)
        + [pl.BlockSpec((1, rows, cols), lambda c, i, h: (c, 0, 0))] * len(rhs)
        + ([] if add is None else [out]),
        sds((planes, depth // 2, cols), BF), out,
        len(lhs) * rows * depth * cols * planes, "weight_half",
    )


def widen_kernel(sec, own0, own1, got0, got1, o):
    half = pl.program_id(1)
    mine = half == sec[0]
    for layer, own, got in ((0, own0, got0), (1, own1, got1)):
        here = sec[0] == layer

        @pl.when(here & mine)
        def _():
            o[...] = own[...].astype(F32)

        @pl.when(here & ~mine)
        def _():
            o[...] = got[...].astype(F32)


def widen(sec, own, got):
    planes, depth, cols = own[0].shape
    blk = min(256, depth)
    n = depth // blk

    def spec(layer, from_own):
        def index_map(c, h, i, s):
            use = (s[0] == layer) & ((h == s[0]) == from_own)
            return (jnp.where(use, c, 0), jnp.where(use, i, 0), 0)

        return pl.BlockSpec((1, blk, cols), index_map)

    return call(
        widen_kernel, (planes, 2, n), (sec,), (*own, *got),
        [spec(0, True), spec(1, True), spec(0, False), spec(1, False)],
        sds((planes, 2 * depth, cols), F32),
        pl.BlockSpec((1, blk, cols), lambda c, h, i, s: (c, h * n + i, 0)),
        own[0].size, "widen", moved=12 * own[0].size,
    )


def swap_sections(x):
    return lax.ppermute(x, "section", [(0, 1), (1, 0)])


def shift_ctx(x, by):
    length = lax.axis_size("ctx")
    return lax.ppermute(
        x, "ctx", [(i, i + by) for i in range(length) if 0 <= i + by < length]
    )


def rope_tables(positions, width):
    half = ROT // 2
    frequency = 10000.0 ** (-(2.0 * jnp.arange(half, dtype=F32)) / ROT)
    angles = positions.astype(F32)[:, None] * frequency[None, :]
    c, s = jnp.cos(angles), jnp.sin(angles)
    zero = jnp.zeros_like(c)
    one = jnp.ones_like(c)

    def lay(*parts):
        head = jnp.concatenate(parts, axis=1)
        return jnp.tile(head, (1, width // HEAD))

    return lay(c, c, one, one), lay(s, zero, zero, zero), lay(zero, s, zero, zero)


def on_device(
    inputs,
    segments,
    cotangent,
    ln_gain,
    ln_bias,
    qkv_weight,
    qkv_bias,
    dense_weight,
    fc1_weight,
    fc1_bias,
    fc2_weight,
    out_bias,
):
    sections = lax.axis_size("section")
    section = lax.axis_index("section")
    ctx_id = lax.axis_index("ctx")
    ctx = lax.axis_size("ctx")
    batches, r, width = inputs.shape
    rows = r * lax.axis_size("tp")
    total_rows = rows * ctx
    local = qkv_weight.shape[3]
    hidden = fc1_weight.shape[2]
    mine = batches // sections
    back = (total_rows // 2) // rows
    blocks = min(back, ctx - 1) + 1
    first_mb = section * mine
    layers = (0, 1)

    small = jnp.concatenate(
        [ln_gain[0], ln_bias[0], out_bias[0], qkv_bias[0].reshape(-1), fc1_bias[0]]
    )
    small_other = swap_sections(small)
    w_own = (qkv_weight[0], fc1_weight[0], dense_weight[0], fc2_weight[0])
    w_other = tuple(swap_sections(w) for w in w_own)
    sel, gain, shift, obias, qkv_b, fc1_b = [], [], [], [], [], []
    for layer in layers:
        sel.append((section != layer).astype(jnp.int32).reshape(1))
        v = jnp.where(section == layer, small, small_other).astype(F32)
        gain.append(v[:width].reshape(1, width))
        shift.append(v[width : 2 * width].reshape(1, width))
        obias.append(v[2 * width : 3 * width].reshape(1, width))
        qkv_b.append(v[3 * width : 3 * width + 3 * local].reshape(3, 1, local))
        fc1_b.append(v[3 * width + 3 * local :].reshape(1, hidden))

    positions = ctx_id * rows + jnp.arange(rows, dtype=jnp.int32)
    wide = rope_tables(positions, min(256, local))
    tables = tuple(t[:, :PAIR] for t in wide)

    docs = lax.dynamic_slice_in_dim(segments, first_mb, mine, 0)
    padded = jnp.pad(docs, ((0, 0), ((blocks - 1) * rows, 0)), constant_values=-1)
    window = lax.dynamic_slice_in_dim(padded, ctx_id * rows, blocks * rows, 1)
    window = window.reshape(mine, blocks, rows)[:, ::-1]
    drow = [window[m, 0].reshape(1, rows) for m in range(mine)]
    dcol = [window[m].reshape(blocks * rows, 1) for m in range(mine)]

    x_in = lax.dynamic_slice_in_dim(inputs, first_mb, mine, 0)
    g_in = lax.dynamic_slice_in_dim(cotangent, first_mb, mine, 0)

    def gather(v):
        return lax.all_gather(v, "tp", axis=0, tiled=True)

    def scatter(v):
        return lax.psum_scatter(v, "tp", scatter_dimension=0, tiled=True)

    qw, fw, dw, ow = zip(w_own, w_other)
    kept = {}
    x = [x_in[m] for m in range(mine)]
    normed = [norm_first(x[m], gain[0], shift[0]) for m in range(mine)]
    outs = []
    for layer in layers:
        branch = []
        for m in range(mine):
            full = gather(normed[m])
            q, kv = project(sel[layer], full, *qw, qkv_b[layer], wide)
            kvs = [kv] + [shift_ctx(kv, j) for j in range(1, blocks)]
            gelu, slope = expand(sel[layer], full, *fw, fc1_b[layer])
            attended, lse = attend(q, kvs, drow[m], dcol[m])
            branch.append(
                scatter(contract(sel[layer], attended, gelu, dw[0], ow[0], dw[1], ow[1]))
            )
            kept[layer, m] = (x[m], full, q, kvs, gelu, slope, attended, lse)
        if layer + 1 < len(layers):
            pairs = [
                norm_next(x[m], branch[m], obias[layer], gain[layer + 1], shift[layer + 1])
                for m in range(mine)
            ]
            x = [p[0] for p in pairs]
            normed = [p[1] for p in pairs]
            outs.append(jnp.stack(x))
        else:
            outs.append(
                jnp.stack(
                    [
                        (x[m].astype(F32) + branch[m].astype(F32) + obias[layer]).astype(BF)
                        for m in range(mine)
                    ]
                )
            )

    g = [g_in[m] for m in range(mine)]
    gin = {}
    sums = {}
    biases = {}
    halves = {}
    keep_half = section.astype(jnp.int32).reshape(1)
    send_half = 1 - keep_half
    for layer in reversed(layers):
        gfull = [gather(g[m]) for m in range(mine)]
        up, qkv_g, gx = [], [], []
        rowsum, bq, bu = 0.0, 0.0, 0.0
        for m in range(mine):
            x_l, full, q, kvs, gelu, slope, attended, lse = kept[layer, m]
            ga = spread_attn(sel[layer], gfull[m], *dw)
            back_out = attend_back(q, kvs, ga, lse, drow[m], dcol[m], tables)
            got = [shift_ctx(back_out[1 + j], -j) for j in range(1, blocks)]
            u, usum = spread_up(sel[layer], gfull[m], *ow, slope)
            p = join(back_out[0], back_out[1], got, tables)
            partial, qsum = gather_grad(sel[layer], p, u, qw[0], fw[0], qw[1], fw[1])
            gx_m, s = norm_back(x_l, scatter(partial), g[m], gain[layer])
            up.append(u)
            qkv_g.append(p)
            gx.append(gx_m)
            rowsum, bq, bu = rowsum + s, bq + qsum, bu + usum
        sums[layer] = rowsum
        biases[layer] = jnp.concatenate([bq.reshape(-1), bu.reshape(-1)])
        fulls = [kept[layer, m][1] for m in range(mine)]
        attn = [kept[layer, m][6] for m in range(mine)]
        gelus = [kept[layer, m][4] for m in range(mine)]
        gplane = [v[None] for v in gfull]
        uplane = [v[None] for v in up]
        jobs = ((attn, gplane), (gelus, gplane), (fulls, uplane), (fulls, qkv_g))
        reduced = []
        for lhs, rhs in jobs:
            got = swap_sections(weight_half(send_half, lhs, rhs))
            reduced.append(lax.psum(weight_half(keep_half, lhs, rhs, got), "ctx"))
        halves[layer] = reduced
        g = gx
        gin[layer] = jnp.stack(gx)

    def to_owner(pair_of):
        moved = swap_sections(jnp.where(section == 0, pair_of[1], pair_of[0]))
        own = jnp.where(section == 0, pair_of[0], pair_of[1])
        return jnp.where(
            section == 0,
            jnp.concatenate([own, moved], axis=0),
            jnp.concatenate([moved, own], axis=0),
        )

    layer_out = to_owner(outs)
    grad_in = to_owner([gin[0], gin[1]])

    final = []
    for k in range(4):
        own = [halves[layer][k] for layer in layers]
        got = [
            lax.ppermute(own[layer], "section", [(1 - layer, layer)]) for layer in layers
        ]
        final.append(widen(keep_half, own, got))
    dense_g, fc2_g, fc1_g, qkv_gr = final

    rowsum = lax.psum(jnp.stack([sums[0], sums[1]]), ("section", "ctx", "tp"))
    rowsum = jnp.where(section == 0, rowsum[0], rowsum[1])
    bias_sum = lax.psum(jnp.stack([biases[0], biases[1]]), ("section", "ctx"))
    bias_sum = jnp.where(section == 0, bias_sum[0], bias_sum[1])

    return (
        layer_out[None],
        grad_in[None],
        rowsum[0][None],
        rowsum[1][None],
        qkv_gr[None],
        bias_sum[: 3 * local].reshape(3, local)[None],
        dense_g,
        fc1_g,
        bias_sum[3 * local :][None],
        fc2_g,
        rowsum[2][None],
    )


def solution(mesh):
    return jax.shard_map(
        on_device,
        mesh=mesh,
        in_specs=(
            P(None, ("ctx", "tp"), None),
            P(),
            P(None, ("ctx", "tp"), None),
            P("section", None),
            P("section", None),
            P("section", None, None, "tp"),
            P("section", None, "tp"),
            P("section", "tp", None),
            P("section", None, "tp"),
            P("section", "tp"),
            P("section", "tp", None),
            P("section", None),
        ),
        out_specs=(
            P("section", None, ("ctx", "tp"), None),
            P("section", None, ("ctx", "tp"), None),
            P("section", None),
            P("section", None),
            P("section", None, None, "tp"),
            P("section", None, "tp"),
            P("section", "tp", None),
            P("section", None, "tp"),
            P("section", "tp"),
            P("section", "tp", None),
            P("section", None),
        ),
        check_vma=False,
    )
```

time: 2310 us -> 1380 us (0.60)
  waiting for transfers between devices: 1210 us -> 703 us
  matrix products: 483 us -> 0 us
  Pallas kernels: 0 us -> 470 us
  local copies, waits for them, and re-layouts: 269 us -> 22.8 us
  other arithmetic: 261 us -> 17 us
  starting transfers between devices: 18.7 us -> 73.9 us
  blocking collectives: 36 us -> 64.9 us
    dot_general x65 -> x0, matrix products: 483 us -> none  [the longest x5 93.2 us: on_device(): lax.dot_general(lax.all_gather(backward_normed_b, 'tp', axis=0, tiled=Tru...]
    pallas_call x0 -> x64, Pallas kernels: none -> 470 us  [call(): pl.pallas_call(kernel, grid_spec=pltpu.PrefetchScalarGridSpec(num_scalar_...]
    all_gather x35 -> x8, waiting for transfers between devices: 499 us -> 73.3 us  [gather(): return lax.all_gather(v, 'tp', axis=0, tiled=True)]
    reduce_scatter x15 -> x8, waiting for transfers between devices: 288 us -> 152 us  [scatter(): return lax.psum_scatter(v, 'tp', scatter_dimension=0, tiled=True)]
    slice x58 -> x18, local copies, waits for them, and re-layouts: 88.1 us -> 7.38 us  [the longest x3 1.99 us: on_device(): tables = tuple((t[:, :PAIR] for t in wide))]
    dynamic_update_slice x49 -> x0, other arithmetic: 71.1 us -> none  [put_slot(): lax.dynamic_update_index_in_dim(buffer, jnp.where(active, leaf_value, tak...]
    ppermute x8 -> x39, waiting for transfers between devices: 10.4 us -> 78.1 us  [the longest x16 49.9 us: shift_ctx(): lax.ppermute(x, 'ctx', [(i, i + by) for i in range(length) if 0 <= i + by...]
    ppermute x8 -> x39, starting transfers between devices: 12.6 us -> 72.6 us  [the longest x16 40.1 us: shift_ctx(): lax.ppermute(x, 'ctx', [(i, i + by) for i in range(length) if 0 <= i + by...]
  transfers between devices with their start and end apart: 59 -> 56, of which waited for: 48 -> 18; matrix products, arithmetic and copies ran while one was open for 26% -> 2% of each run, Pallas kernels for 0% -> 33%
where the time goes in v1:
time: 1380 us; the launch traced here: 1370 us
  waiting for transfers between devices  703 us (51%)
  Pallas kernels  470 us (34%)
  starting transfers between devices  73.9 us (5%)
  blocking collectives  64.9 us (5%)
  local copies, waits for them, and re-layouts  22.8 us (2%)
  other arithmetic  17 us (1%)
  between operations  15.1 us (1%)
    pallas_call x64, Pallas kernels, call(): pl.pallas_call(kernel, grid_spec=pltpu.PrefetchScalarGridSpec(num_scalar_...  470 us
    psum x1, waiting for transfers between devices, on_device(): reduced.append(lax.psum(weight_half(keep_half, lhs, rhs, got), 'ctx'))  399 us
    reduce_scatter x8, waiting for transfers between devices, scatter(): return lax.psum_scatter(v, 'tp', scatter_dimension=0, tiled=True)  152 us
    all_gather x8, waiting for transfers between devices, gather(): return lax.all_gather(v, 'tp', axis=0, tiled=True)  73.3 us
    ppermute x16, waiting for transfers between devices, shift_ctx(): lax.ppermute(x, 'ctx', [(i, i + by) for i in range(length) if 0 <= i + by...  49.9 us
    ppermute x16, starting transfers between devices, shift_ctx(): lax.ppermute(x, 'ctx', [(i, i + by) for i in range(length) if 0 <= i + by...  40.1 us
    psum x1, blocking collectives, on_device(): rowsum = lax.psum(jnp.stack([sums[0], sums[1]]), ('section', 'ctx', 'tp'))  38.4 us
    ppermute x15, waiting for transfers between devices, swap_sections(): return lax.ppermute(x, 'section', [(0, 1), (1, 0)])  28.2 us
  transfers between devices with their start and end apart: 56, of which 18 were waited for; matrix products, arithmetic and copies ran while one was open for 2% of the time, Pallas kernels for 33%

profile of v1, /device:TPU:0, one launch (start us, length us, event | category | flops | bytes accessed | tf_op | source)
XLA Modules:
  0.0 1366.5 jit_solution(14673693432148276705)
XLA Ops:
  14.5 27.4 %collective-permute-done = bf16[9728]{0:T(1024)(128)(2,1)S(1)} collective-permute-done((bf16[9728]{0:T(1024)(128)(2,1)S(1)}, bf16[9728]{0:T(1024)(128)(2,1)S(1)}, u32[]{:S(2)}, u32[]{:S(2)}) %collective-permute-start) | collective-permute-done | bytes 19488 | tf_op jit(solution)/shard_map/ppermute | solution.py:545
  50.7 24.6 %all-gather.11.cloned.1.call-done.x.refs_0_ = bf16[256,2048]{1,0:T(8,128)(2,1)} async-done(((bf16[64,2048]{1,0:T(8,128)(2,1)}), bf16[256,2048]{1,0:T(8,128)(2,1)}) %all-gather.11.cloned.1.call-update) | async-done | bytes 1048592 | tf_op jit(solution)/shard_map/all_gather | solution.py:630
  75.3 8.3 project.4
  92.9 16.5 %collective-permute-done.3.refs_5_.refs_10_ = bf16[2,256,512]{2,1,0:T(8,128)(2,1)S(1)} collective-permute-done((bf16[2,256,512]{2,1,0:T(8,128)(2,1)}, bf16[2,256,512]{2,1,0:T(8,128)(2,1)S(1)}, u32[]{:S(2)}, u32[]{:S(2)}) %collective-permute-start.3) | collective-permute-done | bytes 524320 | tf_op jit(solution)/shard_map/ppermute | solution.py:550
  117.1 9.8 expand.4
  128.2 10.1 contract.4
  138.4 8.3 project.5
  153.4 19.6 %collective-permute-done.8.refs_5_.refs_10_ = bf16[2,256,512]{2,1,0:T(8,128)(2,1)S(1)} collective-permute-done((bf16[2,256,512]{2,1,0:T(8,128)(2,1)}, bf16[2,256,512]{2,1,0:T(8,128)(2,1)S(1)}, u32[]{:S(2)}, u32[]{:S(2)}) %collective-permute-start.8) | collective-permute-done | bytes 524320 | tf_op jit(solution)/shard_map/ppermute | solution.py:550
  180.9 9.8 expand.5
  190.7 10.2 contract.5
  204.9 23.9 %reduce-scatter.11.cloned.1.call-done.branch = bf16[64,2048]{1,0:T(8,128)(2,1)} async-done(((bf16[256,2048]{1,0:T(8,128)(2,1)}), bf16[64,2048]{1,0:T(8,128)(2,1)}) %reduce-scatter.11.cloned.1.call-update) | async-done | bytes 262160 | tf_op jit(solution)/shard_map/reduce_scatter | solution.py:633
  231.6 25.7 %all-gather.15.cloned.1.call-done.x.refs_0_ = bf16[256,2048]{1,0:T(8,128)(2,1)} async-done(((bf16[64,2048]{1,0:T(8,128)(2,1)}), bf16[256,2048]{1,0:T(8,128)(2,1)}) %all-gather.15.cloned.1.call-update) | async-done | bytes 1048592 | tf_op jit(solution)/shard_map/all_gather | solution.py:630
  257.3 8.6 project.6
  274.8 11.3 all-gather.23.cloned.1.call-done.refs_2_
  299.2 9.7 attend_back.4
  311.4 10.1 expand.6
  321.6 9.8 spread_up.4
  336.4 11.9 gather_grad.4
  348.5 8.5 project.7
  370.1 12.1 collective-permute-done.12.refs_5_.refs_10_
  390.0 9.7 attend_back.6
  402.3 10.1 expand.7
  412.4 9.6 spread_up.6
  427.1 11.9 gather_grad.6
  441.6 27.8 %reduce-scatter.21.cloned.1.call-done.gn = bf16[64,2048]{1,0:T(8,128)(2,1)} async-done(((bf16[256,2048]{1,0:T(8,128)(2,1)}), bf16[64,2048]{1,0:T(8,128)(2,1)}) %reduce-scatter.21.cloned.1.call-update) | async-done | bytes 262160 | tf_op jit(solution)/shard_map/reduce_scatter | solution.py:633
  471.9 10.4 weight_half.18
  500.8 9.7 attend_back.5
  529.8 9.7 attend_back.7
  548.6 9.3 spread_up.5
  557.9 9.3 spread_up.7
  583.1 10.3 weight_half.16
  602.1 10.7 weight_half.19
  619.9 7.1 weight_half.27
  630.8 10.7 weight_half.17
  655.9 10.3 contract.6
  666.3 10.1 contract.7
  676.5 12.9 gather_grad.5
  689.8 12.5 gather_grad.7
  702.3 399.1 %all-reduce.5.cloned.1.call-done = (bf16[3,1024,512]{2,1,0:T(8,128)(2,1)}, bf16[3,1024,512]{2,1,0:T(8,128)(2,1)}, bf16[1,256,2048]{2,1,0:T(8,128)(2,1)}, bf16[1,...) async-done(((bf16[3,1024,512]{2,1,0:T(8,128)(2,1)}, ...) | async-done | bytes 25165840 | tf_op jit(solution)/shard_map/psum | solution.py:705
  1110.7 21.5 %reduce-scatter.13.cloned.1.call-done = bf16[64,2048]{1,0:T(8,128)(2,1)} async-done(((bf16[256,2048]{1,0:T(8,128)(2,1)}), bf16[64,2048]{1,0:T(8,128)(2,1)}) %reduce-scatter.13.cloned.1.call-update) | async-done | bytes 262160 | tf_op jit(solution)/shard_map/reduce_scatter | solution.py:633
  1132.2 28.5 %reduce-scatter.15.cloned.1.call-done = bf16[64,2048]{1,0:T(8,128)(2,1)} async-done(((bf16[256,2048]{1,0:T(8,128)(2,1)}), bf16[64,2048]{1,0:T(8,128)(2,1)}) %reduce-scatter.15.cloned.1.call-update) | async-done | bytes 262160 | tf_op jit(solution)/shard_map/reduce_scatter | solution.py:633
  1164.1 24.5 %reduce-scatter.19.cloned.1.call-done.gn = bf16[64,2048]{1,0:T(8,128)(2,1)} async-done(((bf16[256,2048]{1,0:T(8,128)(2,1)}), bf16[64,2048]{1,0:T(8,128)(2,1)}) %reduce-scatter.19.cloned.1.call-update) | async-done | bytes 262160 | tf_op jit(solution)/shard_map/reduce_scatter | solution.py:633
  1191.0 25.6 %reduce-scatter.23.cloned.1.call-done.gn = bf16[64,2048]{1,0:T(8,128)(2,1)} async-done(((bf16[256,2048]{1,0:T(8,128)(2,1)}), bf16[64,2048]{1,0:T(8,128)(2,1)}) %reduce-scatter.23.cloned.1.call-update) | async-done | bytes 262160 | tf_op jit(solution)/shard_map/reduce_scatter | solution.py:633
  1246.3 26.5 %psum.73 = f32[2,3584]{1,0:T(2,128)S(1)} all-reduce(f32[2,3584]{1,0:T(2,128)S(1)} %pad_maximum_fusion.5), channel_id=1, replica_groups=mesh['section'=2,'ctx'=4,'tp'=4] {'section','ctx'}, use_global_device_ids=true, to_apply=%region_11.12 | all-reduce | flops 7168 | bytes 57344 | tf_op jit(solution)/shard_map/psum | solution.py:733
  1274.1 38.4 %psum.70 = f32[2,3,2048]{2,1,0:T(4,128)S(1)} all-reduce(f32[2,3,2048]{2,1,0:T(4,128)S(1)} %pad_maximum_fusion.4), channel_id=1, replica_groups=mesh['section'=2,'ctx'=4,'tp'=4] {'section','ctx','tp'}, use_global_device_ids=true, to_apply=%region_8.9 | all-reduce | flops 12288 | bytes 98304 | tf_op jit(solution)/shard_map/psum | solution.py:731
  1320.2 16.4 %widen.4 = f32[3,2048,512]{2,1,0:T(8,128)} custom-call(s32[1]{0:T(128)} %bitcast.40.half.sec, bf16[3,1024,512]{2,1,0:T(8,128)(2,1)} %get-tuple-element.149.own0, bf16[3,1024,512]{2,1,0:T(8,128)(2,1)} %get-tuple-element.150.own1, bf16[3,1024,512]{2,1,0:T(8,128)(2,1)} %collective-permute-done.25.got0, bf16[3,1024,512]{2,1,0:T(8,128)(2,1)} %collective-permute-done.26.got1), custom_call_target="tpu_custom_call" | custom-call | flops 1572864 | bytes 18874368 | tf_op jit(solution)/shard_map/widen/pallas_call | solution.py:35
  1336.7 11.4 widen.6
  1348.1 11.4 widen.7
  (282 shorter events, 269.6 us)
Async XLA Ops:
  7.2 68.1 %all-gather.11.cloned.1.call-start = ((), (), s32[]{:S(2)}) async-start(), calls=%async_computation.8 | async-start | bytes 1310720 | tf_op jit(solution)/shard_map/all_gather | solution.py:630
  7.2 109.8 %collective-permute-start.4 = (bf16[2048,2048]{1,0:T(8,128)(2,1)}, bf16[2048,2048]{1,0:T(8,128)(2,1)}, u32[]{:S(2)}, u32[]{:S(2)}) collective-permute-start(bf16[2048,2048]{1,0:T(8,128)(2,1)} %bitcast.80), channel_id=1, source_target_pairs={{0,16},{16,0},{1,17},{17,1},{2,18},{18,2},{3,19},{19,3},{4,20},{20... | collective-permute-start | bytes 25165832 | tf_op jit(solution)/shard_map/ppermute | solution.py:545
  7.8 119.1 %collective-permute-start.6 = (bf16[2048,2048]{1,0:T(8,128)(2,1)}, bf16[2048,2048]{1,0:T(8,128)(2,1)}, u32[]{:S(2)}, u32[]{:S(2)}) collective-permute-start(bf16[2048,2048]{1,0:T(8,128)(2,1)} %bitcast.71), channel_id=1, source_target_pairs={{0,16},{16,0},{1,17},{17,1},{2,18},{18,2},{3,19},{19,3},{4,20},{20... | collective-permute-start | bytes 25165832 | tf_op jit(solution)/shard_map/ppermute | solution.py:545
  7.9 67.4 %collective-permute-start.1 = (bf16[3,2048,512]{2,1,0:T(8,128)(2,1)}, bf16[3,2048,512]{2,1,0:T(8,128)(2,1)}, u32[]{:S(2)}, u32[]{:S(2)}) collective-permute-start(bf16[3,2048,512]{2,1,0:T(8,128)(2,1)} %bitcast.89), channel_id=1, source_target_pairs={{0,16},{16,0},{1,17},{17,1},{2,18},{18,2},{3,19},{19,3},{4,20},{20... | collective-permute-start | bytes 18874376 | tf_op jit(solution)/shard_map/ppermute | solution.py:545
  12.5 29.4 %collective-permute-start = (bf16[9728]{0:T(1024)(128)(2,1)S(1)}, bf16[9728]{0:T(1024)(128)(2,1)S(1)}, u32[]{:S(2)}, u32[]{:S(2)}) collective-permute-start(bf16[9728]{0:T(1024)(128)(2,1)S(1)} %dynamic-update-slice.4), channel_id=1, source_target_pairs={{0,16},{16,0},{1,17},{17,1},{2,18},{18,2},{3,19},{19,3},{4,20},{20... | collective-permute-start | bytes 58376 | tf_op jit(solution)/shard_map/ppermute | solution.py:545
  44.5 93.9 %all-gather.13.cloned.1.call-start = ((), (), s32[]{:S(2)}) async-start(), calls=%async_computation.10 | async-start | bytes 1310720 | tf_op jit(solution)/shard_map/all_gather | solution.py:630
  44.6 82.3 %collective-permute-start.5 = (bf16[512,2048]{1,0:T(8,128)(2,1)}, bf16[512,2048]{1,0:T(8,128)(2,1)S(1)}, u32[]{:S(2)}, u32[]{:S(2)}) collective-permute-start(bf16[512,2048]{1,0:T(8,128)(2,1)} %bitcast.98), channel_id=1, source_target_pairs={{0,16},{16,0},{1,17},{17,1},{2,18},{18,2},{3,19},{19,3},{4,20},{20... | collective-permute-start | bytes 6291464 | tf_op jit(solution)/shard_map/ppermute | solution.py:545
  47.2 154.7 %reduce-scatter.9.cloned.1.call-start = ((), (), s32[]{:S(2)}) async-start(), calls=%async_computation.9 | async-start | bytes 1310720 | tf_op jit(solution)/shard_map/reduce_scatter | solution.py:633
  83.5 25.9 %collective-permute-start.3 = (bf16[2,256,512]{2,1,0:T(8,128)(2,1)}, bf16[2,256,512]{2,1,0:T(8,128)(2,1)S(1)}, u32[]{:S(2)}, u32[]{:S(2)}) collective-permute-start(bf16[2,256,512]{2,1,0:T(8,128)(2,1)} %get-tuple-element.80.refs_3_.refs_8_), channel_id=1, source_target_pairs={{0,8},{4,12},{1,9},{5,13},{2,10},{6,14},{3,11},{7,15},{16,24},{20,... | collective-permute-start | bytes 1572872 | tf_op jit(solution)/shard_map/ppermute | solution.py:550
  138.3 90.5 %reduce-scatter.11.cloned.1.call-start = ((), (), s32[]{:S(2)}) async-start(), calls=%async_computation.11 | async-start | bytes 1310720 | tf_op jit(solution)/shard_map/reduce_scatter | solution.py:633
  146.7 26.3 %collective-permute-start.8 = (bf16[2,256,512]{2,1,0:T(8,128)(2,1)}, bf16[2,256,512]{2,1,0:T(8,128)(2,1)S(1)}, u32[]{:S(2)}, u32[]{:S(2)}) collective-permute-start(bf16[2,256,512]{2,1,0:T(8,128)(2,1)} %get-tuple-element.85.refs_3_.refs_8_), channel_id=1, source_target_pairs={{0,8},{4,12},{1,9},{5,13},{2,10},{6,14},{3,11},{7,15},{16,24},{20,... | collective-permute-start | bytes 1572872 | tf_op jit(solution)/shard_map/ppermute | solution.py:550
  201.0 56.4 %all-gather.15.cloned.1.call-start = ((), (), s32[]{:S(2)}) async-start(), calls=%async_computation.12 | async-start | bytes 1310720 | tf_op jit(solution)/shard_map/all_gather | solution.py:630
  204.0 82.2 %all-gather.23.cloned.1.call-start = ((), (), s32[]{:S(2)}) async-start(), calls=%async_computation.22 | async-start | bytes 1310720 | tf_op jit(solution)/shard_map/all_gather | solution.py:630
  204.9 143.6 %all-gather.17.cloned.1.call-start = ((), (), s32[]{:S(2)}) async-start(), calls=%async_computation.14 | async-start | bytes 1310720 | tf_op jit(solution)/shard_map/all_gather | solution.py:630
  230.9 135.6 %all-gather.25.cloned.1.call-start = ((), (), s32[]{:S(2)}) async-start(), calls=%async_computation.23 | async-start | bytes 1310720 | tf_op jit(solution)/shard_map/all_gather | solution.py:630
  265.9 25.4 %collective-permute-start.10 = (bf16[2,256,512]{2,1,0:T(8,128)(2,1)}, bf16[2,256,512]{2,1,0:T(8,128)(2,1)S(1)}, u32[]{:S(2)}, u32[]{:S(2)}) collective-permute-start(bf16[2,256,512]{2,1,0:T(8,128)(2,1)} %get-tuple-element.91.refs_3_.refs_8_), channel_id=1, source_target_pairs={{0,8},{4,12},{1,9},{5,13},{2,10},{6,14},{3,11},{7,15},{16,24},{20,... | collective-permute-start | bytes 1572872 | tf_op jit(solution)/shard_map/ppermute | solution.py:550
  272.7 166.4 %reduce-scatter.17.cloned.1.call-start = ((), (), s32[]{:S(2)}) async-start(), calls=%async_computation.16 | async-start | bytes 1310720 | tf_op jit(solution)/shard_map/reduce_scatter | solution.py:633
  308.8 22.5 %collective-permute-start.14 = (bf16[2,256,512]{2,1,0:T(8,128)(2,1)}, bf16[2,256,512]{2,1,0:T(8,128)(2,1)S(1)}, u32[]{:S(2)}, u32[]{:S(2)}) collective-permute-start(bf16[2,256,512]{2,1,0:T(8,128)(2,1)} %get-tuple-element.102), channel_id=1, source_target_pairs={{4,0},{8,4},{12,8},{5,1},{9,5},{13,9},{6,2},{10,6},{14,10},{7,3},{... | collective-permute-start | bytes 1572872 | tf_op jit(solution)/shard_map/ppermute | solution.py:550
  348.4 120.9 %reduce-scatter.21.cloned.1.call-start = ((), (), s32[]{:S(2)}) async-start(), calls=%async_computation.19 | async-start | bytes 1310720 | tf_op jit(solution)/shard_map/reduce_scatter | solution.py:633
  357.0 25.2 %collective-permute-start.12 = (bf16[2,256,512]{2,1,0:T(8,128)(2,1)}, bf16[2,256,512]{2,1,0:T(8,128)(2,1)S(1)}, u32[]{:S(2)}, u32[]{:S(2)}) collective-permute-start(bf16[2,256,512]{2,1,0:T(8,128)(2,1)} %get-tuple-element.96.refs_3_.refs_8_), channel_id=1, source_target_pairs={{0,8},{4,12},{1,9},{5,13},{2,10},{6,14},{3,11},{7,15},{16,24},{20,... | collective-permute-start | bytes 1572872 | tf_op jit(solution)/shard_map/ppermute | solution.py:550
  439.1 58.2 %all-gather.19.cloned.1.call-start = ((), (), s32[]{:S(2)}) async-start(), calls=%async_computation.17 | async-start | bytes 1310720 | tf_op jit(solution)/shard_map/all_gather | solution.py:630
  441.5 84.8 %all-gather.21.cloned.1.call-start = ((), (), s32[]{:S(2)}) async-start(), calls=%async_computation.20 | async-start | bytes 1310720 | tf_op jit(solution)/shard_map/all_gather | solution.py:630
  471.7 629.7 %all-reduce.5.cloned.1.call-start = ((), (), s32[]{:S(2)}) async-start(), calls=%async_computation.24 | async-start | bytes 50331648 | tf_op jit(solution)/shard_map/psum | solution.py:705
  482.3 111.1 %collective-permute-start.24 = (bf16[3,1024,512]{2,1,0:T(8,128)(2,1)}, bf16[3,1024,512]{2,1,0:T(8,128)(2,1)S(1)}, u32[]{:S(2)}, u32[]{:S(2)}) collective-permute-start(bf16[3,1024,512]{2,1,0:T(8,128)(2,1)} %weight_half.18), channel_id=1, source_target_pairs={{0,16},{16,0},{1,17},{17,1},{2,18},{18,2},{3,19},{19,3},{4,20},{20... | collective-permute-start | bytes 9437192 | tf_op jit(solution)/shard_map/ppermute | solution.py:545
  485.7 53.8 %collective-permute-start.28 = (bf16[1,256,2048]{2,1,0:T(8,128)(2,1)}, bf16[1,256,2048]{2,1,0:T(8,128)(2,1)}, u32[]{:S(2)}, u32[]{:S(2)}) collective-permute-start(bf16[1,256,2048]{2,1,0:T(8,128)(2,1)} %weight_half.22), channel_id=1, source_target_pairs={{0,16},{16,0},{1,17},{17,1},{2,18},{18,2},{3,19},{19,3},{4,20},{20... | collective-permute-start | bytes 3145736 | tf_op jit(solution)/shard_map/ppermute | solution.py:545
  492.5 105.5 %collective-permute-start.36 = (bf16[1,1024,2048]{2,1,0:T(8,128)(2,1)}, bf16[1,1024,2048]{2,1,0:T(8,128)(2,1)}, u32[]{:S(2)}, u32[]{:S(2)}) collective-permute-start(bf16[1,1024,2048]{2,1,0:T(8,128)(2,1)} %weight_half.30), channel_id=1, source_target_pairs={{0,16},{16,0},{1,17},{17,1},{2,18},{18,2},{3,19},{19,3},{4,20},{20... | collective-permute-start | bytes 12582920 | tf_op jit(solution)/shard_map/ppermute | solution.py:545
  510.5 36.6 %collective-permute-start.16 = (bf16[2,256,512]{2,1,0:T(8,128)(2,1)}, bf16[2,256,512]{2,1,0:T(8,128)(2,1)}, u32[]{:S(2)}, u32[]{:S(2)}) collective-permute-start(bf16[2,256,512]{2,1,0:T(8,128)(2,1)} %get-tuple-element.111), channel_id=1, source_target_pairs={{4,0},{8,4},{12,8},{5,1},{9,5},{13,9},{6,2},{10,6},{14,10},{7,3},{... | collective-permute-start | bytes 1572872 | tf_op jit(solution)/shard_map/ppermute | solution.py:550
  511.8 35.3 %collective-permute-start.17 = (bf16[2,256,512]{2,1,0:T(8,128)(2,1)}, bf16[2,256,512]{2,1,0:T(8,128)(2,1)}, u32[]{:S(2)}, u32[]{:S(2)}) collective-permute-start(bf16[2,256,512]{2,1,0:T(8,128)(2,1)} %get-tuple-element.112), channel_id=1, source_target_pairs={{8,0},{12,4},{9,1},{13,5},{10,2},{14,6},{11,3},{15,7},{24,16},{28,... | collective-permute-start | bytes 1572872 | tf_op jit(solution)/shard_map/ppermute | solution.py:550
  539.5 27.7 %collective-permute-start.20 = (bf16[2,256,512]{2,1,0:T(8,128)(2,1)}, bf16[2,256,512]{2,1,0:T(8,128)(2,1)S(1)}, u32[]{:S(2)}, u32[]{:S(2)}) collective-permute-start(bf16[2,256,512]{2,1,0:T(8,128)(2,1)} %get-tuple-element.129), channel_id=1, source_target_pairs={{4,0},{8,4},{12,8},{5,1},{9,5},{13,9},{6,2},{10,6},{14,10},{7,3},{... | collective-permute-start | bytes 1572872 | tf_op jit(solution)/shard_map/ppermute | solution.py:550
  547.1 72.9 %collective-permute-start.32 = (bf16[1,1024,2048]{2,1,0:T(8,128)(2,1)}, bf16[1,1024,2048]{2,1,0:T(8,128)(2,1)}, u32[]{:S(2)}, u32[]{:S(2)}) collective-permute-start(bf16[1,1024,2048]{2,1,0:T(8,128)(2,1)} %weight_half.26), channel_id=1, source_target_pairs={{0,16},{16,0},{1,17},{17,1},{2,18},{18,2},{3,19},{19,3},{4,20},{20... | collective-permute-start | bytes 12582920 | tf_op jit(solution)/shard_map/ppermute | solution.py:545
  547.1 27.5 %collective-permute-start.21 = (bf16[2,256,512]{2,1,0:T(8,128)(2,1)}, bf16[2,256,512]{2,1,0:T(8,128)(2,1)}, u32[]{:S(2)}, u32[]{:S(2)}) collective-permute-start(bf16[2,256,512]{2,1,0:T(8,128)(2,1)} %get-tuple-element.130), channel_id=1, source_target_pairs={{8,0},{12,4},{9,1},{13,5},{10,2},{14,6},{11,3},{15,7},{24,16},{28,... | collective-permute-start | bytes 1572872 | tf_op jit(solution)/shard_map/ppermute | solution.py:550
  567.2 74.3 %collective-permute-start.35 = (bf16[1,1024,2048]{2,1,0:T(8,128)(2,1)}, bf16[1,1024,2048]{2,1,0:T(8,128)(2,1)}, u32[]{:S(2)}, u32[]{:S(2)}) collective-permute-start(bf16[1,1024,2048]{2,1,0:T(8,128)(2,1)} %weight_half.28), channel_id=1, source_target_pairs={{0,16},{16,0},{1,17},{17,1},{2,18},{18,2},{3,19},{19,3},{4,20},{20... | collective-permute-start | bytes 12582920 | tf_op jit(solution)/shard_map/ppermute | solution.py:545
  574.7 74.0 %collective-permute-start.31 = (bf16[1,1024,2048]{2,1,0:T(8,128)(2,1)}, bf16[1,1024,2048]{2,1,0:T(8,128)(2,1)}, u32[]{:S(2)}, u32[]{:S(2)}) collective-permute-start(bf16[1,1024,2048]{2,1,0:T(8,128)(2,1)} %weight_half.24), channel_id=1, source_target_pairs={{0,16},{16,0},{1,17},{17,1},{2,18},{18,2},{3,19},{19,3},{4,20},{20... | collective-permute-start | bytes 12582920 | tf_op jit(solution)/shard_map/ppermute | solution.py:545
  593.5 37.4 %collective-permute-start.23 = (bf16[3,1024,512]{2,1,0:T(8,128)(2,1)}, bf16[3,1024,512]{2,1,0:T(8,128)(2,1)}, u32[]{:S(2)}, u32[]{:S(2)}) collective-permute-start(bf16[3,1024,512]{2,1,0:T(8,128)(2,1)} %weight_half.16), channel_id=1, source_target_pairs={{0,16},{16,0},{1,17},{17,1},{2,18},{18,2},{3,19},{19,3},{4,20},{20... | collective-permute-start | bytes 9437192 | tf_op jit(solution)/shard_map/ppermute | solution.py:545
  597.9 29.1 %collective-permute-start.27 = (bf16[1,256,2048]{2,1,0:T(8,128)(2,1)}, bf16[1,256,2048]{2,1,0:T(8,128)(2,1)}, u32[]{:S(2)}, u32[]{:S(2)}) collective-permute-start(bf16[1,256,2048]{2,1,0:T(8,128)(2,1)} %weight_half.20), channel_id=1, source_target_pairs={{0,16},{16,0},{1,17},{17,1},{2,18},{18,2},{3,19},{19,3},{4,20},{20... | collective-permute-start | bytes 3145736 | tf_op jit(solution)/shard_map/ppermute | solution.py:545
  655.8 476.3 %reduce-scatter.13.cloned.1.call-start = ((), (), s32[]{:S(2)}) async-start(), calls=%async_computation.13 | async-start | bytes 1310720 | tf_op jit(solution)/shard_map/reduce_scatter | solution.py:633
  666.2 494.5 %reduce-scatter.15.cloned.1.call-start = ((), (), s32[]{:S(2)}) async-start(), calls=%async_computation.15 | async-start | bytes 1310720 | tf_op jit(solution)/shard_map/reduce_scatter | solution.py:633
  676.4 512.2 %reduce-scatter.19.cloned.1.call-start = ((), (), s32[]{:S(2)}) async-start(), calls=%async_computation.18 | async-start | bytes 1310720 | tf_op jit(solution)/shard_map/reduce_scatter | solution.py:633
  689.5 527.1 %reduce-scatter.23.cloned.1.call-start = ((), (), s32[]{:S(2)}) async-start(), calls=%async_computation.21 | async-start | bytes 1310720 | tf_op jit(solution)/shard_map/reduce_scatter | solution.py:633
  1101.4 141.9 %collective-permute-start.25 = (bf16[3,1024,512]{2,1,0:T(8,128)(2,1)}, bf16[3,1024,512]{2,1,0:T(8,128)(2,1)}, u32[]{:S(2)}, u32[]{:S(2)}) collective-permute-start(bf16[3,1024,512]{2,1,0:T(8,128)(2,1)} %get-tuple-element.149.own0), channel_id=1, source_target_pairs={{16,0},{17,1},{18,2},{19,3},{20,4},{21,5},{22,6},{23,7},{24,8},{25... | collective-permute-start | bytes 9437192 | tf_op jit(solution)/shard_map/ppermute | solution.py:726
  1102.7 126.6 %collective-permute-start.29 = (bf16[1,256,2048]{2,1,0:T(8,128)(2,1)}, bf16[1,256,2048]{2,1,0:T(8,128)(2,1)}, u32[]{:S(2)}, u32[]{:S(2)}) collective-permute-start(bf16[1,256,2048]{2,1,0:T(8,128)(2,1)} %get-tuple-element.151.own0), channel_id=1, source_target_pairs={{16,0},{17,1},{18,2},{19,3},{20,4},{21,5},{22,6},{23,7},{24,8},{25... | collective-permute-start | bytes 3145736 | tf_op jit(solution)/shard_map/ppermute | solution.py:726
  1104.0 126.6 %collective-permute-start.30 = (bf16[1,256,2048]{2,1,0:T(8,128)(2,1)}, bf16[1,256,2048]{2,1,0:T(8,128)(2,1)}, u32[]{:S(2)}, u32[]{:S(2)}) collective-permute-start(bf16[1,256,2048]{2,1,0:T(8,128)(2,1)} %get-tuple-element.152.own1), channel_id=1, source_target_pairs={{0,16},{1,17},{2,18},{3,19},{4,20},{5,21},{6,22},{7,23},{8,24},{9,... | collective-permute-start | bytes 3145736 | tf_op jit(solution)/shard_map/ppermute | solution.py:726
  1164.1 56.8 %collective-permute-start.13 = (bf16[2,64,2048]{2,1,0:T(8,128)(2,1)}, bf16[2,64,2048]{2,1,0:T(8,128)(2,1)}, u32[]{:S(2)}, u32[]{:S(2)}) collective-permute-start(bf16[2,64,2048]{2,1,0:T(8,128)(2,1)} %get-tuple-element.162), channel_id=1, source_target_pairs={{0,16},{16,0},{1,17},{17,1},{2,18},{18,2},{3,19},{19,3},{4,20},{20... | collective-permute-start | bytes 1572872 | tf_op jit(solution)/shard_map/ppermute | solution.py:545
  1220.9 115.7 %collective-permute-start.33 = (bf16[1,1024,2048]{2,1,0:T(8,128)(2,1)}, bf16[1,1024,2048]{2,1,0:T(8,128)(2,1)}, u32[]{:S(2)}, u32[]{:S(2)}) collective-permute-start(bf16[1,1024,2048]{2,1,0:T(8,128)(2,1)} %get-tuple-element.153.own0), channel_id=1, source_target_pairs={{16,0},{17,1},{18,2},{19,3},{20,4},{21,5},{22,6},{23,7},{24,8},{25... | collective-permute-start | bytes 12582920 | tf_op jit(solution)/shard_map/ppermute | solution.py:726
  1223.0 113.7 %collective-permute-start.34 = (bf16[1,1024,2048]{2,1,0:T(8,128)(2,1)}, bf16[1,1024,2048]{2,1,0:T(8,128)(2,1)}, u32[]{:S(2)}, u32[]{:S(2)}) collective-permute-start(bf16[1,1024,2048]{2,1,0:T(8,128)(2,1)} %get-tuple-element.154.own1), channel_id=1, source_target_pairs={{0,16},{1,17},{2,18},{3,19},{4,20},{5,21},{6,22},{7,23},{8,24},{9,... | collective-permute-start | bytes 12582920 | tf_op jit(solution)/shard_map/ppermute | solution.py:726
  1229.3 118.7 %collective-permute-start.37 = (bf16[1,1024,2048]{2,1,0:T(8,128)(2,1)}, bf16[1,1024,2048]{2,1,0:T(8,128)(2,1)}, u32[]{:S(2)}, u32[]{:S(2)}) collective-permute-start(bf16[1,1024,2048]{2,1,0:T(8,128)(2,1)} %get-tuple-element.155.own0), channel_id=1, source_target_pairs={{16,0},{17,1},{18,2},{19,3},{20,4},{21,5},{22,6},{23,7},{24,8},{25... | collective-permute-start | bytes 12582920 | tf_op jit(solution)/shard_map/ppermute | solution.py:726
  1230.6 117.5 %collective-permute-start.38 = (bf16[1,1024,2048]{2,1,0:T(8,128)(2,1)}, bf16[1,1024,2048]{2,1,0:T(8,128)(2,1)}, u32[]{:S(2)}, u32[]{:S(2)}) collective-permute-start(bf16[1,1024,2048]{2,1,0:T(8,128)(2,1)} %get-tuple-element.156.own1), channel_id=1, source_target_pairs={{0,16},{1,17},{2,18},{3,19},{4,20},{5,21},{6,22},{7,23},{8,24},{9,... | collective-permute-start | bytes 12582920 | tf_op jit(solution)/shard_map/ppermute | solution.py:726
  1243.4 76.9 %collective-permute-start.26 = (bf16[3,1024,512]{2,1,0:T(8,128)(2,1)S(1)}, bf16[3,1024,512]{2,1,0:T(8,128)(2,1)}, u32[]{:S(2)}, u32[]{:S(2)}) collective-permute-start(bf16[3,1024,512]{2,1,0:T(8,128)(2,1)S(1)} %copy-done.7), channel_id=1, source_target_pairs={{0,16},{1,17},{2,18},{3,19},{4,20},{5,21},{6,22},{7,23},{8,24},{9,... | collective-permute-start | bytes 9437192 | tf_op jit(solution)/shard_map/ppermute | solution.py:726
  (38 other events, 4096.5 us)
Sparse Core Ops, SparseCore 0:
  44.7 30.5 all-gather.10
  77.4 27.3 all-gather.12
  138.5 27.2 reduce-scatter.8
  201.1 27.6 reduce-scatter.10
  230.8 26.4 all-gather.14
  258.7 27.3 all-gather.22
  287.7 27.3 all-gather.16
  316.7 27.4 all-gather.24
  348.5 30.2 reduce-scatter.16
  439.2 30.0 reduce-scatter.20
  470.9 26.3 all-gather.18
  498.7 27.5 all-gather.20
  656.0 445.4 all-reduce.4
  1104.1 27.9 reduce-scatter.12
  1134.9 25.7 reduce-scatter.14
  1162.8 25.7 reduce-scatter.18
  1190.8 25.7 reduce-scatter.22

commit v2 on v1

--- a/solution.py
+++ b/solution.py
@@ -60,22 +60,63 @@
     return pl.BlockSpec(shape, lambda *_: (0,) * len(shape))
 
 
-def picked(shape, which, index):
-    def index_map(*args):
-        ids, sel = args[:-1], args[-1]
-        return tuple(jnp.where(sel[0] == which, i, 0) for i in index(*ids))
-
-    return pl.BlockSpec(shape, index_map)
-
-
-def on_pick(sel, own, other, body):
-    @pl.when(sel[0] == 0)
-    def _():
-        body(*own)
-
-    @pl.when(sel[0] != 0)
-    def _():
-        body(*other)
+def stream(name, sel, xs, weights, n, extra, extra_specs, outs, out_specs, body, flops):
+    nx, nw, ne, no = len(xs), len(weights), len(extra), len(outs)
+
+    def kernel(*refs):
+        pick_ref, refs = refs[0], refs[1:]
+        x_refs, refs = refs[:nx], refs[nx:]
+        own, refs = refs[:nw], refs[nw:]
+        other, refs = refs[:nw], refs[nw:]
+        extra_refs, refs = refs[:ne], refs[ne:]
+        out_refs, refs = refs[:no], refs[no:]
+        x_buf, refs = refs[:nx], refs[nx:]
+        w_buf, (x_sem, w_sem) = refs[:nw], refs[nw:]
+        j = pl.program_id(0)
+
+        def weight_copy(side, k, i):
+            return pltpu.make_async_copy(
+                weights[k][3](side[k], i), w_buf[k].at[i], w_sem.at[k, i]
+            )
+
+        @pl.when(j == 0)
+        def _():
+            copies = [
+                pltpu.make_async_copy(x_refs[i], x_buf[i], x_sem.at[i]) for i in range(nx)
+            ]
+            for c in copies:
+                c.start()
+
+            @pl.when(pick_ref[0] == 0)
+            def _():
+                for i in range(n):
+                    for k in range(nw):
+                        weight_copy(own, k, i).start()
+
+            @pl.when(pick_ref[0] != 0)
+            def _():
+                for i in range(n):
+                    for k in range(nw):
+                        weight_copy(other, k, i).start()
+
+            for c in copies:
+                c.wait()
+
+        for k in range(nw):
+            weight_copy(own, k, j).wait()
+        body(j, x_buf, [w_buf[k].at[j] for k in range(nw)], extra_refs, out_refs)
+
+    own = [w[0] for w in weights]
+    other = [w[1] for w in weights]
+    hbm = pl.BlockSpec(memory_space=pl.ANY)
+    scratch = [pltpu.VMEM(x.shape, x.dtype) for x in xs]
+    scratch += [pltpu.VMEM((n,) + tuple(w[2]), BF) for w in weights]
+    scratch += [pltpu.SemaphoreType.DMA((nx,)), pltpu.SemaphoreType.DMA((nw, n))]
+    return call(
+        kernel, (n,), (sel,), (*xs, *own, *other, *extra),
+        [hbm] * (nx + 2 * nw) + list(extra_specs), outs, out_specs, flops, name,
+        scratch=scratch, moved=nbytes(*xs, *own, *extra) + nbytes(*outs),
+    )
 
 
 def center(x):
@@ -147,111 +188,97 @@
     return a * cosine + (down - up if sign > 0 else up - down)
 
 
-def project_kernel(sel, x, own, other, bias, cosine, low, high, q, kv):
-    step = pl.program_id(0)
-
-    def body(w):
-        a = dot(x[...], w[0]) + bias[0]
-
-        @pl.when(step == 0)
-        def _():
-            kv[0] = turn(a, cosine[...], low[...], high[...], 1).astype(BF)
-
-        @pl.when(step == 1)
-        def _():
-            kv[0] = a.astype(BF)
-
-        @pl.when(step == 2)
-        def _():
-            q[...] = turn(a, cosine[...], low[...], high[...], 1).astype(BF)
-
-    on_pick(sel, (own,), (other,), body)
-
-
 def project(sel, x, own, other, bias, tables):
     rows, width = x.shape
     local = own.shape[2]
-    blk = min(256, local)
-    n = local // blk
-
-    def w_index(c, j):
-        return (lax.rem(c + 1, 3), 0, j)
-
-    table = whole((rows, blk))
-    return call(
-        project_kernel, (3, n), (sel,), (x, own, other, bias, *tables),
-        [
-            whole(x.shape),
-            picked((1, width, blk), 0, w_index),
-            picked((1, width, blk), 1, w_index),
-            pl.BlockSpec((1, 1, blk), lambda c, j, s: (lax.rem(c + 1, 3), 0, j)),
-            table, table, table,
-        ],
+
+    def body(j, xs, ws, extra, out):
+        bias_ref, cosine, low, high = extra
+        q, kv = out
+        a = dot(xs[0][...], ws[0][...]) + bias_ref[0]
+
+        def turned(to):
+            for p in range(0, local, PAIR):
+                piece = turn(a[:, p : p + PAIR], cosine[...], low[...], high[...], 1)
+                to[:, p : p + PAIR] = piece.astype(BF)
+
+        @pl.when(j == 0)
+        def _():
+            turned(kv.at[0])
+
+        @pl.when(j == 1)
+        def _():
+            kv[0] = a.astype(BF)
+
+        @pl.when(j == 2)
+        def _():
+            turned(q)
+
+    table = whole((rows, PAIR))
+    return stream(
+        "project", sel, [x],
+        [(own, other, (width, local), lambda w, i: w.at[lax.rem(i + 1, 3)])], 3,
+        (bias, *tables),
+        [pl.BlockSpec((1, 1, local), lambda j, s: (lax.rem(j + 1, 3), 0, 0))] + [table] * 3,
         (sds((rows, local), BF), sds((2, rows, local), BF)),
         (
-            pl.BlockSpec((rows, blk), lambda c, j, s: (0, jnp.where(c == 2, j, 0))),
-            pl.BlockSpec(
-                (1, rows, blk),
-                lambda c, j, s: (jnp.minimum(c, 1), 0, jnp.where(c == 2, n - 1, j)),
-            ),
+            whole((rows, local)),
+            pl.BlockSpec((1, rows, local), lambda j, s: (jnp.minimum(j, 1), 0, 0)),
         ),
-        6 * rows * width * local, "project", moved=nbytes(own, x) + 6 * rows * local,
-    )
-
-
-def expand_kernel(sel, x, own, other, bias, gelu, slope):
-    def body(w):
-        u = dot(x[...], w[...]) + bias[...]
+        body, 6 * rows * width * local,
+    )
+
+
+def columns(blk):
+    return lambda w, i: w.at[:, pl.ds(pl.multiple_of(i * blk, blk), blk)]
+
+
+def lines(blk):
+    return lambda w, i: w.at[pl.ds(pl.multiple_of(i * blk, blk), blk)]
+
+
+def expand(sel, x, own, other, bias):
+    rows, width = x.shape
+    hidden = own.shape[1]
+    blk = 512
+
+    def body(j, xs, ws, extra, out):
+        u = dot(xs[0][...], ws[0][...]) + extra[0][...]
         t = jnp.tanh(GELU_ROOT * (u + GELU_CUBE * u * u * u))
-        gelu[...] = (0.5 * u * (1.0 + t)).astype(BF)
-        slope[...] = (
+        out[0][...] = (0.5 * u * (1.0 + t)).astype(BF)
+        out[1][...] = (
             0.5 * (1.0 + t)
             + 0.5 * u * (1.0 - t * t) * GELU_ROOT * (1.0 + 3.0 * GELU_CUBE * u * u)
         ).astype(BF)
 
-    on_pick(sel, (own,), (other,), body)
-
-
-def expand(sel, x, own, other, bias):
-    rows, width = x.shape
-    hidden = own.shape[1]
-    blk = 256
-    out = pl.BlockSpec((rows, blk), lambda j, s: (0, j))
-    return call(
-        expand_kernel, (hidden // blk,), (sel,), (x, own, other, bias),
-        [
-            whole(x.shape),
-            picked((width, blk), 0, lambda j: (0, j)),
-            picked((width, blk), 1, lambda j: (0, j)),
-            pl.BlockSpec((1, blk), lambda j, s: (0, j)),
-        ],
-        (sds((rows, hidden), BF), sds((rows, hidden), BF)), (out, out),
-        2 * rows * width * hidden, "expand", moved=nbytes(own, x) + 4 * rows * hidden,
-    )
-
-
-def contract_kernel(sel, a, u, d_own, f_own, d_other, f_other, o):
-    def body(d, f):
-        o[...] = (dot(a[...], d[...]) + dot(u[...], f[...])).astype(BF)
-
-    on_pick(sel, (d_own, f_own), (d_other, f_other), body)
+    spec = pl.BlockSpec((rows, blk), lambda j, s: (0, j))
+    return stream(
+        "expand", sel, [x], [(own, other, (width, blk), columns(blk))], hidden // blk,
+        (bias,), [pl.BlockSpec((1, blk), lambda j, s: (0, j))],
+        (sds((rows, hidden), BF), sds((rows, hidden), BF)), (spec, spec),
+        body, 2 * rows * width * hidden,
+    )
 
 
 def contract(sel, a, u, d_own, f_own, d_other, f_other):
     rows, local = a.shape
     hidden = u.shape[1]
     width = d_own.shape[1]
-    blk = 256
-    specs = [
-        picked((k, blk), which, lambda j: (0, j)) for which in (0, 1) for k in (local, hidden)
-    ]
-    return call(
-        contract_kernel, (width // blk,), (sel,), (a, u, d_own, f_own, d_other, f_other),
-        [whole(a.shape), whole(u.shape)] + specs,
-        sds((rows, width), BF), pl.BlockSpec((rows, blk), lambda j, s: (0, j)),
-        2 * rows * (local + hidden) * width, "contract",
-        moved=nbytes(a, u, d_own, f_own) + 2 * rows * width,
-    )
+    blk = 512
+
+    def body(j, xs, ws, extra, out):
+        out[0][...] = (dot(xs[0][...], ws[0][...]) + dot(xs[1][...], ws[1][...])).astype(BF)
+
+    return stream(
+        "contract", sel, [a, u],
+        [
+            (d_own, d_other, (local, blk), columns(blk)),
+            (f_own, f_other, (hidden, blk), columns(blk)),
+        ],
+        width // blk, (), [],
+        (sds((rows, width), BF),), (pl.BlockSpec((rows, blk), lambda j, s: (0, j)),),
+        body, 2 * rows * (local + hidden) * width,
+    )[0]
 
 
 def masks_of(blocks, rows, drow, dcol):
@@ -376,107 +403,88 @@
     gq, own = refs[0], refs[1]
     got = refs[2 : 2 + count]
     cosine, low, high, out = refs[2 + count :]
-    gk = sum((r[0].astype(F32) for r in got), own[0])
-    gv = sum((r[1].astype(F32) for r in got), own[1])
     out[0] = gq[...]
-    out[1] = turn(gk, cosine[...], low[...], high[...], -1).astype(BF)
-    out[2] = gv.astype(BF)
+    out[2] = sum((r[1].astype(F32) for r in got), own[1]).astype(BF)
+    for p in range(0, gq.shape[1], PAIR):
+        at = slice(p, p + PAIR)
+        gk = sum((r[0, :, at].astype(F32) for r in got), own[0, :, at])
+        out[1, :, at] = turn(gk, cosine[...], low[...], high[...], -1).astype(BF)
 
 
 def join(gq, own, got, tables):
     rows, local = gq.shape
-    two = pl.BlockSpec((2, rows, PAIR), lambda p: (0, 0, p))
-    table = pl.BlockSpec((rows, PAIR), lambda p: (0, 0))
     return call(
-        functools.partial(join_kernel, len(got)), (local // PAIR,), (), (gq, own, *got, *tables),
-        [pl.BlockSpec((rows, PAIR), lambda p: (0, p)), two] + [two] * len(got) + [table] * 3,
-        sds((3, rows, local), BF), pl.BlockSpec((3, rows, PAIR), lambda p: (0, 0, p)),
-        10 * own.size, "join",
-    )
-
-
-def spread_attn_kernel(sel, g, own, other, o):
-    def body(w):
-        o[...] = dot(g[...], w[...], NT).astype(BF)
-
-    on_pick(sel, (own,), (other,), body)
+        functools.partial(join_kernel, len(got)), (1,), (), (gq, own, *got, *tables),
+        [whole(gq.shape), whole(own.shape)]
+        + [whole(own.shape)] * len(got)
+        + [whole((rows, PAIR))] * 3,
+        sds((3, rows, local), BF), whole((3, rows, local)), 10 * own.size, "join",
+    )
 
 
 def spread_attn(sel, g, own, other):
     rows, width = g.shape
     local = own.shape[0]
     blk = min(256, local)
-    return call(
-        spread_attn_kernel, (local // blk,), (sel,), (g, own, other),
-        [
-            whole(g.shape),
-            picked((blk, width), 0, lambda j: (j, 0)),
-            picked((blk, width), 1, lambda j: (j, 0)),
-        ],
-        sds((rows, local), BF), pl.BlockSpec((rows, blk), lambda j, s: (0, j)),
-        2 * rows * width * local, "spread_attn", moved=nbytes(g, own) + 2 * rows * local,
-    )
-
-
-def spread_up_kernel(sel, g, own, other, slope, o, sums):
-    def body(w):
-        u = (dot(g[...], w[...], NT) * slope[...].astype(F32)).astype(BF)
-        o[...] = u
-        sums[...] = jnp.sum(u.astype(F32), axis=0, keepdims=True)
-
-    on_pick(sel, (own,), (other,), body)
+
+    def body(j, xs, ws, extra, out):
+        out[0][...] = dot(xs[0][...], ws[0][...], NT).astype(BF)
+
+    return stream(
+        "spread_attn", sel, [g], [(own, other, (blk, width), lines(blk))], local // blk,
+        (), [], (sds((rows, local), BF),),
+        (pl.BlockSpec((rows, blk), lambda j, s: (0, j)),), body, 2 * rows * width * local,
+    )[0]
 
 
 def spread_up(sel, g, own, other, slope):
     rows, width = g.shape
     hidden = own.shape[0]
-    blk = 256
+    blk = 512
+
+    def body(j, xs, ws, extra, out):
+        u = (dot(xs[0][...], ws[0][...], NT) * extra[0][...].astype(F32)).astype(BF)
+        out[0][...] = u
+        out[1][...] = jnp.sum(u.astype(F32), axis=0, keepdims=True)
+
     col = pl.BlockSpec((rows, blk), lambda j, s: (0, j))
-    return call(
-        spread_up_kernel, (hidden // blk,), (sel,), (g, own, other, slope),
-        [
-            whole(g.shape),
-            picked((blk, width), 0, lambda j: (j, 0)),
-            picked((blk, width), 1, lambda j: (j, 0)),
-            col,
-        ],
-        (sds((rows, hidden), BF), sds((1, hidden), F32)),
-        (col, pl.BlockSpec((1, blk), lambda j, s: (0, j))),
-        2 * rows * width * hidden, "spread_up", moved=nbytes(g, own, slope) + 2 * rows * hidden,
-    )
-
-
-def gather_grad_kernel(sel, qkv, up, w_own, f_own, w_other, f_other, o, sums):
-    def body(w, f):
-        a = dot(up[...], f[...], NT)
-        for c in range(3):
-            a += dot(qkv[c], w[c], NT)
-        o[...] = a.astype(BF)
-
-    on_pick(sel, (w_own, f_own), (w_other, f_other), body)
-
-    @pl.when(pl.program_id(0) == 0)
-    def _():
-        for c in range(3):
-            sums[c : c + 1, :] = jnp.sum(qkv[c].astype(F32), axis=0, keepdims=True)
+    return stream(
+        "spread_up", sel, [g], [(own, other, (blk, width), lines(blk))], hidden // blk,
+        (slope,), [col], (sds((rows, hidden), BF), sds((1, hidden), F32)),
+        (col, pl.BlockSpec((1, blk), lambda j, s: (0, j))), body, 2 * rows * width * hidden,
+    )
 
 
 def gather_grad(sel, qkv, up, w_own, f_own, w_other, f_other):
     _, rows, local = qkv.shape
     hidden = up.shape[1]
     width = f_own.shape[0]
-    blk = 256
-    specs = []
-    for which in (0, 1):
-        specs.append(picked((3, blk, local), which, lambda j: (0, j, 0)))
-        specs.append(picked((blk, hidden), which, lambda j: (j, 0)))
-    return call(
-        gather_grad_kernel, (width // blk,), (sel,), (qkv, up, w_own, f_own, w_other, f_other),
-        [whole(qkv.shape), whole(up.shape)] + specs,
+    blk = 512
+
+    def body(j, xs, ws, extra, out):
+        a = dot(xs[1][...], ws[1][...], NT)
+        for c in range(3):
+            a += dot(xs[0][c], ws[0][c], NT)
+        out[0][...] = a.astype(BF)
+
+        @pl.when(j == 0)
+        def _():
+            for c in range(3):
+                out[1][c : c + 1, :] = jnp.sum(xs[0][c].astype(F32), axis=0, keepdims=True)
+
+    return stream(
+        "gather_grad", sel, [qkv, up],
+        [
+            (
+                w_own, w_other, (3, blk, local),
+                lambda w, i: w.at[:, pl.ds(pl.multiple_of(i * blk, blk), blk)],
+            ),
+            (f_own, f_other, (blk, hidden), lines(blk)),
+        ],
+        width // blk, (), [],
         (sds((rows, width), BF), sds((3, local), F32)),
         (pl.BlockSpec((rows, blk), lambda j, s: (0, j)), whole((3, local))),
-        2 * rows * width * (3 * local + hidden), "gather_grad",
-        moved=nbytes(qkv, up, w_own, f_own) + 2 * rows * width,
+        body, 2 * rows * width * (3 * local + hidden),
     )
 
 
@@ -541,8 +549,258 @@
     )
 
 
+TILE = (128, 512)
+
+
+def wide_kernel(count, adds, *refs):
+    place, refs = refs[0], refs[1:]
+    lhs, rhs = refs[:count], refs[count : 2 * count]
+    total = refs[-1]
+    a = 0.0
+    for x, y in zip(lhs, rhs):
+        a += dot(x[...], y[...].reshape(y.shape[-2:]), TN)
+    total[...] = a.reshape(total.shape)
+    add = refs[2 * count] if adds else None
+    outs = refs[-5:-1] if adds else refs[-2:-1]
+    x, y = place[1], place[2]
+    for c in range(2):
+        for a_rel in range(2):
+            for b_rel in range(2):
+                a_abs = a_rel ^ (x if c == 0 else y)
+                b_abs = b_rel ^ (y if c == 0 else x)
+                k = 4 * c + 2 * a_abs + b_abs
+                for t in range(total.shape[2] // TILE[1]):
+                    at = slice(TILE[1] * t, TILE[1] * (t + 1))
+                    v = total[k, :, at]
+                    if adds:
+                        v = v + add[c, a_rel, b_rel, t].astype(F32)
+                        outs[2 * c + a_rel][b_rel, t] = v.astype(BF)
+                    else:
+                        outs[0][c, a_rel, b_rel, t] = v.astype(BF)
+
+
+def dense_kernel(count, adds, *refs):
+    place, refs = refs[0], refs[1:]
+    lhs, rhs = refs[:count], refs[count : 2 * count]
+    total = refs[-1]
+    a = 0.0
+    for x, y in zip(lhs, rhs):
+        a += dot(x[...], y[...], TN)
+    for rb in range(2):
+        for t in range(4):
+            total[4 * rb + t] = a[128 * rb : 128 * (rb + 1), TILE[1] * t : TILE[1] * (t + 1)]
+    add = refs[2 * count] if adds else None
+    outs = refs[-5:-1] if adds else refs[-2:-1]
+    x, y = place[1], place[2]
+    for c in range(2):
+        for a_rel in range(2):
+            for b_rel in range(2):
+                a_abs = a_rel ^ (x if c == 0 else y)
+                b_abs = b_rel ^ (y if c == 0 else x)
+                v = total[4 * c + 2 * a_abs + b_abs]
+                if adds:
+                    v = v + add[c, a_rel, b_rel, 0].astype(F32)
+                    outs[2 * c + a_rel][b_rel, 0] = v.astype(BF)
+                else:
+                    outs[0][c, a_rel, b_rel, 0] = v.astype(BF)
+
+
+def wide_part(kind, tiles, offset, place, lhs, rhs, add, base):
+    rows, depth = lhs[0].shape
+    if kind == "qkv":
+        grid, step_tiles, cols = (3,), 1, 512
+        rhs_spec = pl.BlockSpec((1, rows, cols), lambda n, h: (n, 0, 0))
+    elif kind == "dense":
+        grid, step_tiles, cols = (1,), 1, 2048
+        rhs_spec = pl.BlockSpec((rows, cols), lambda n, h: (0, 0))
+    else:
+        step_tiles = 2 if offset % 2 == 0 else 1
+        cols = 512 * step_tiles
+        grid = (rhs[0].shape[1] // cols,)
+        rhs_spec = pl.BlockSpec((rows, cols), lambda n, h: (0, n))
+    lhs_spec = pl.BlockSpec((rows, depth // 2), lambda n, h: (0, h[0]))
+    first = offset // step_tiles
+    one = pl.BlockSpec((2, 2, 2, step_tiles) + TILE, lambda n, h: (0, 0, 0, first + n, 0, 0))
+    four = pl.BlockSpec((2, step_tiles) + TILE, lambda n, h: (0, first + n, 0, 0))
+    ins = [*lhs, *rhs]
+    specs = [lhs_spec] * len(lhs) + [rhs_spec] * len(rhs)
+    if add is None:
+        outs, out_specs = [sds((2, 2, 2, tiles) + TILE, BF)], [one]
+    else:
+        ins.append(add)
+        specs.append(one)
+        outs, out_specs = [sds((2, tiles) + TILE, BF)] * 4, [four] * 4
+    aliases = {}
+    if base is not None:
+        for i, b in enumerate(base):
+            aliases[1 + len(ins)] = i
+            ins.append(b)
+            specs.append(pl.BlockSpec(memory_space=pl.ANY))
+    kernel = dense_kernel if kind == "dense" else wide_kernel
+    args = (len(lhs), add is not None)
+    width = 512 if kind == "dense" else cols
+
+    def body(*refs):
+        if base is not None:
+            cutoff = 1 + len(ins) - len(base)
+            refs = refs[:cutoff] + refs[1 + len(ins) :]
+        kernel(*args, *refs)
+
+    planes = rhs[0].size // rows
+    return pl.pallas_call(
+        body,
+        grid_spec=pltpu.PrefetchScalarGridSpec(
+            num_scalar_prefetch=1, grid=grid, in_specs=specs, out_specs=out_specs,
+            scratch_shapes=[pltpu.VMEM((8, 128, width), F32)],
+        ),
+        out_shape=outs,
+        input_output_aliases=aliases,
+        name="wide_" + kind,
+        cost_estimate=pl.CostEstimate(
+            flops=len(lhs) * rows * depth * planes,
+            bytes_accessed=nbytes(*lhs) // 2 + nbytes(*rhs) + depth * planes * 2,
+            transcendentals=0,
+        ),
+        compiler_params=pltpu.CompilerParams(vmem_limit_bytes=VMEM_LIMIT),
+    )(place, *ins)
+
+
+def group_half(parts, place, add=None):
+    tiles = sum(p[1] for p in parts)
+    base, offset = None, 0
+    for kind, count, lhs, rhs in parts:
+        base = wide_part(kind, tiles, offset, place, lhs, rhs, add, base)
+        offset += count
+    return base
+
+
+def plus(*xs):
+    return sum(x.astype(F32) for x in xs).astype(BF)
+
+
+def hop(x, axis_bit):
+    return lax.ppermute(x, "ctx", [(i, i ^ axis_bit) for i in range(4)])
+
+
+def hop_in(x, axis_bit, layer):
+    pairs = [(4 * layer + i, 4 * layer + (i ^ axis_bit)) for i in range(4)]
+    return lax.ppermute(x, ("section", "ctx"), pairs)
+
+
+def reduce_group(parts, layer, keep, send, order):
+    base = group_half(order(parts), send)
+    got = swap_sections(base[0])
+    yield base[0]
+    k0, s0, k1, s1 = group_half(order(parts), keep, got)
+    r0, r1 = hop(s0, 1), hop(s1, 2)
+    yield k0
+    t0, t1 = plus(k0[1], r0[1]), plus(k1[1], r1[1])
+    q0, q1 = hop(t0, 2), hop(t1, 1)
+    yield t0
+    f = jnp.stack([plus(k0[0], r0[0], q0), plus(k1[0], r1[0], q1)])
+    other = lax.ppermute(f, "section", [(1 - layer, layer)])
+    yield f
+    full = jnp.stack([f, other] if layer == 0 else [other, f], axis=1)
+    fx, fy = hop_in(full, 1, layer), hop_in(full, 2, layer)
+    yield full
+    d0, d1 = hop_in(fy[0], 1, layer), hop_in(fx[1], 2, layer)
+    yield full, fx, fy, d0, d1
+
+
+def widen_group_kernel(kinds, counts, *refs):
+    sec = refs[0]
+    step = pl.program_id(0)
+    ins = refs[2:12]
+    outs = refs[12:]
+    starts = (0, 4, 8, 12, 14, 16)
+
+    for layer in (0, 1):
+        for k in range(5):
+            src = ins[5 * layer + k]
+
+            @pl.when((sec[0] == layer) & (step >= starts[k]) & (step < starts[k + 1]))
+            def _(src=src):
+                offset = 0
+                for kind, count, out in zip(kinds, counts, outs):
+                    for t in range(count):
+                        tile = src[0, 0, offset + t].astype(F32)
+                        if kind == "qkv":
+                            out[t] = tile
+                        elif kind == "dense":
+                            out[...] = tile
+                        else:
+                            out[:, TILE[1] * t : TILE[1] * (t + 1)] = tile
+                    offset += count
+
+
+def widen_group(parts, sec, order, pieces):
+    kinds = tuple(p[0] for p in parts)
+    counts = tuple(p[1] for p in parts)
+    tiles = sum(counts)
+    specs, ins = [], []
+    for layer in (0, 1):
+        start = 0
+        for piece in pieces[layer]:
+            arr = piece.reshape((-1, 1, tiles) + TILE)
+            n = arr.shape[0]
+
+            def index_map(i, s, o, layer=layer, start=start, n=n):
+                at = jnp.clip(i - start, 0, n - 1)
+                return (jnp.where(s[0] == layer, at, 0), 0, 0, 0, 0)
+
+            ins.append(arr)
+            specs.append(pl.BlockSpec((1, 1, tiles) + TILE, index_map))
+            start += n
+    outs, out_specs = [], []
+    for kind, count in zip(kinds, counts):
+        if kind == "qkv":
+            outs.append(sds((3, 2048, 512), F32))
+            out_specs.append(pl.BlockSpec((3, 128, 512), lambda i, s, o: (0, o[i], 0)))
+        elif kind == "dense":
+            outs.append(sds((512, 2048), F32))
+            out_specs.append(
+                pl.BlockSpec((128, 512), lambda i, s, o: (o[i] // 4, o[i] % 4))
+            )
+        else:
+            outs.append(sds((2048, 2048), F32))
+            out_specs.append(pl.BlockSpec((128, 2048), lambda i, s, o: (o[i], 0)))
+    return pl.pallas_call(
+        functools.partial(widen_group_kernel, kinds, counts),
+        grid_spec=pltpu.PrefetchScalarGridSpec(
+            num_scalar_prefetch=2, grid=(16,), in_specs=specs, out_specs=out_specs
+        ),
+        out_shape=outs,
+        name="widen_group",
+        cost_estimate=pl.CostEstimate(
+            flops=0, bytes_accessed=6 * 16 * tiles * 128 * 512, transcendentals=0
+        ),
+        compiler_params=pltpu.CompilerParams(vmem_limit_bytes=VMEM_LIMIT),
+    )(sec, order, *ins)
+
+
+def class_order(at_x, at_y):
+    order = []
+    for colours, dx, dy in (
+        ((0, 1), 0, 0), ((0, 1), 1, 0), ((0, 1), 0, 1), ((0,), 1, 1), ((1,), 1, 1),
+    ):
+        for c in colours:
+            for h in (0, 1):
+                x, y = at_x ^ dx, at_y ^ dy
+                a, b = (x, y) if c == 0 else (y, x)
+                order.append(8 * h + 4 * c + 2 * a + b)
+    return jnp.stack(order).astype(jnp.int32)
+
+
 def swap_sections(x):
     return lax.ppermute(x, "section", [(0, 1), (1, 0)])
+
+
+def butterfly(x, axis):
+    length, bit = lax.axis_size(axis), 1
+    while bit < length:
+        x = x + lax.ppermute(x, axis, [(i, i ^ bit) for i in range(length)])
+        bit *= 2
+    return x
 
 
 def shift_ctx(x, by):
@@ -595,13 +853,16 @@
     blocks = min(back, ctx - 1) + 1
     first_mb = section * mine
     layers = (0, 1)
+    square = (ctx, local, hidden, width) == (4, 512, 2048, 2048)
+    at_x, at_y = ctx_id % 2, ctx_id // 2
 
     small = jnp.concatenate(
         [ln_gain[0], ln_bias[0], out_bias[0], qkv_bias[0].reshape(-1), fc1_bias[0]]
     )
     small_other = swap_sections(small)
     w_own = (qkv_weight[0], fc1_weight[0], dense_weight[0], fc2_weight[0])
-    w_other = tuple(swap_sections(w) for w in w_own)
+    ready, _ = lax.optimization_barrier((w_own, small_other))
+    w_other = tuple(swap_sections(w) for w in ready)
     sel, gain, shift, obias, qkv_b, fc1_b = [], [], [], [], [], []
     for layer in layers:
         sel.append((section != layer).astype(jnp.int32).reshape(1))
@@ -613,8 +874,7 @@
         fc1_b.append(v[3 * width + 3 * local :].reshape(1, hidden))
 
     positions = ctx_id * rows + jnp.arange(rows, dtype=jnp.int32)
-    wide = rope_tables(positions, min(256, local))
-    tables = tuple(t[:, :PAIR] for t in wide)
+    tables = rope_tables(positions, PAIR)
 
     docs = lax.dynamic_slice_in_dim(segments, first_mb, mine, 0)
     padded = jnp.pad(docs, ((0, 0), ((blocks - 1) * rows, 0)), constant_values=-1)
@@ -633,79 +893,210 @@
         return lax.psum_scatter(v, "tp", scatter_dimension=0, tiled=True)
 
     qw, fw, dw, ow = zip(w_own, w_other)
-    kept = {}
-    x = [x_in[m] for m in range(mine)]
-    normed = [norm_first(x[m], gain[0], shift[0]) for m in range(mine)]
-    outs = []
-    for layer in layers:
-        branch = []
-        for m in range(mine):
-            full = gather(normed[m])
-            q, kv = project(sel[layer], full, *qw, qkv_b[layer], wide)
-            kvs = [kv] + [shift_ctx(kv, j) for j in range(1, blocks)]
-            gelu, slope = expand(sel[layer], full, *fw, fc1_b[layer])
-            attended, lse = attend(q, kvs, drow[m], dcol[m])
-            branch.append(
-                scatter(contract(sel[layer], attended, gelu, dw[0], ow[0], dw[1], ow[1]))
+    last = [None]
+
+    def after(v):
+        if last[0] is None:
+            return v
+        return lax.optimization_barrier((v, last[0]))[0]
+
+    def mark(out):
+        last[0] = jax.tree.leaves(out)[0]
+        return out
+
+    S = {}
+
+    def project_step(l, m):
+        q, kv = mark(project(sel[l], after(S["full", l, m]), *qw, qkv_b[l], tables))
+        S["q", l, m] = q
+        S["kvs", l, m] = [kv] + [shift_ctx(kv, j) for j in range(1, blocks)]
+
+    def expand_step(l, m):
+        S["gelu", l, m], S["slope", l, m] = mark(
+            expand(sel[l], after(S["full", l, m]), *fw, fc1_b[l])
+        )
+
+    def attend_step(l, m):
+        S["att", l, m], S["lse", l, m] = mark(
+            attend(after(S["q", l, m]), S["kvs", l, m], drow[m], dcol[m])
+        )
+
+    def contract_step(l, m):
+        part = mark(
+            contract(sel[l], after(S["att", l, m]), S["gelu", l, m], dw[0], ow[0], dw[1], ow[1])
+        )
+        S["branch", l, m] = scatter(part)
+
+    def next_step(l, m):
+        S["x", l + 1, m], normed = mark(
+            norm_next(after(S["x", l, m]), S["branch", l, m], obias[l], gain[l + 1], shift[l + 1])
+        )
+        S["full", l + 1, m] = gather(normed)
+
+    def attn_grad_step(l, m):
+        ga = mark(spread_attn(sel[l], after(S["gfull", l, m]), *dw))
+        out = mark(
+            attend_back(
+                after(S["q", l, m]), S["kvs", l, m], ga, S["lse", l, m], drow[m], dcol[m], tables
             )
-            kept[layer, m] = (x[m], full, q, kvs, gelu, slope, attended, lse)
-        if layer + 1 < len(layers):
-            pairs = [
-                norm_next(x[m], branch[m], obias[layer], gain[layer + 1], shift[layer + 1])
-                for m in range(mine)
-            ]
-            x = [p[0] for p in pairs]
-            normed = [p[1] for p in pairs]
-            outs.append(jnp.stack(x))
+        )
+        S["gq", l, m] = out[:2]
+        S["got", l, m] = [shift_ctx(out[1 + j], -j) for j in range(1, blocks)]
+
+    def up_grad_step(l, m):
+        S["up", l, m], S["bu", l, m] = mark(
+            spread_up(sel[l], after(S["gfull", l, m]), *ow, S["slope", l, m])
+        )
+
+    def join_step(l, m):
+        gq, own = S["gq", l, m]
+        S["qkv", l, m] = mark(join(after(gq), own, S["got", l, m], tables))
+
+    def gather_step(l, m):
+        part, S["bq", l, m] = mark(
+            gather_grad(
+                sel[l], after(S["qkv", l, m]), S["up", l, m], qw[0], fw[0], qw[1], fw[1]
+            )
+        )
+        S["gn", l, m] = scatter(part)
+
+    def back_step(l, m):
+        S["gx", l, m], S["sums", l, m] = mark(
+            norm_back(after(S["x", l, m]), S["gn", l, m], S["g", l, m], gain[l])
+        )
+        if l > 0:
+            S["g", l - 1, m] = S["gx", l, m]
+            S["gfull", l - 1, m] = gather(S["gx", l, m])
+
+    def each(name, l):
+        return [S[name, l, m] for m in range(mine)]
+
+    keep_half = section.astype(jnp.int32)
+    place_keep = jnp.stack([keep_half, at_x, at_y]).astype(jnp.int32)
+    place_send = jnp.stack([1 - keep_half, at_x, at_y]).astype(jnp.int32)
+
+    def ordered(parts):
+        (kind, count, lhs, rhs), *rest = parts
+        return [(kind, count, [after(lhs[0]), *lhs[1:]], rhs), *rest]
+
+    def out_parts(l):
+        g = each("gfull", l)
+        return (("fc2", 4, each("gelu", l), g), ("dense", 1, each("att", l), g))
+
+    def in_parts(l):
+        full = each("full", l)
+        return (("fc1", 4, full, each("up", l)), ("qkv", 3, full, each("qkv", l)))
+
+    groups = {}
+
+    def group_step(l, k):
+        if not square:
+            return
+        if (l, k) not in groups:
+            parts = (out_parts, in_parts)[k](l)
+            groups[l, k] = reduce_group(parts, l, place_keep, place_send, ordered)
+        S["group", l, k] = next(groups[l, k])
+        mark(S["group", l, k])
+
+    for m in range(mine):
+        S["x", 0, m] = x_in[m]
+        S["full", 0, m] = gather(mark(norm_first(after(x_in[m]), gain[0], shift[0])))
+    for m in range(mine):
+        project_step(0, m)
+        if m == 0:
+            expand_step(0, 0)
+    for m in range(mine):
+        if m > 0:
+            expand_step(0, m)
+        attend_step(0, m)
+        contract_step(0, m)
+    for m in range(mine):
+        next_step(0, m)
+    held = lax.optimization_barrier((g_in, S["full", 1, mine - 1]))[0]
+    for m in range(mine):
+        S["g", 1, m] = g_in[m]
+        S["gfull", 1, m] = gather(held[m])
+    for m in range(mine):
+        project_step(1, m)
+        if m == 0:
+            expand_step(1, 0)
+    for m in range(mine):
+        if m > 0:
+            expand_step(1, m)
+        attend_step(1, m)
+
+    group_step(1, 0)
+    attn_grad_step(1, 0)
+    group_step(1, 0)
+    for m in range(1, mine):
+        attn_grad_step(1, m)
+    for m in range(mine):
+        up_grad_step(1, m)
+        join_step(1, m)
+        gather_step(1, m)
+        group_step(1, 0) if m < 2 else None
+    group_step(1, 1)
+    group_step(1, 0)
+    group_step(1, 1)
+    for m in range(mine):
+        back_step(1, m)
+    for m in range(mine):
+        contract_step(1, m)
+    group_step(1, 0)
+    attn_grad_step(0, 0)
+    up_grad_step(0, 0)
+    group_step(1, 1)
+    for m in range(1, mine):
+        attn_grad_step(0, m)
+    group_step(0, 0)
+    join_step(0, 0)
+    gather_step(0, 0)
+    group_step(0, 0)
+    for m in range(1, mine):
+        up_grad_step(0, m)
+        join_step(0, m)
+        gather_step(0, m)
+    group_step(1, 1)
+    group_step(0, 1)
+    group_step(1, 1)
+    group_step(0, 1)
+    for m in range(mine):
+        back_step(0, m)
+    group_step(0, 0)
+    group_step(0, 0)
+    group_step(0, 1)
+    group_step(1, 1)
+    group_step(0, 0)
+    group_step(0, 1)
+    group_step(0, 0)
+    group_step(0, 1)
+    group_step(0, 1)
+
+    outs = [jnp.stack(each("x", 1)), None]
+    outs[1] = jnp.stack(
+        [
+            (x.astype(F32) + b.astype(F32) + obias[1]).astype(BF)
+            for x, b in zip(each("x", 1), each("branch", 1))
+        ]
+    )
+    gin = [jnp.stack(each("gx", l)) for l in layers]
+    sums = [sum(each("sums", l)) for l in layers]
+    biases = [
+        jnp.concatenate([sum(each("bq", l)).reshape(-1), sum(each("bu", l)).reshape(-1)])
+        for l in layers
+    ]
+    halves = {}
+    for l in layers:
+        if square:
+            halves[l] = [S["group", l, k] for k in range(2)]
         else:
-            outs.append(
-                jnp.stack(
-                    [
-                        (x[m].astype(F32) + branch[m].astype(F32) + obias[layer]).astype(BF)
-                        for m in range(mine)
-                    ]
+            halves[l] = []
+            for _, _, lhs, rhs in out_parts(l) + in_parts(l):
+                rhs = [v.reshape((-1,) + v.shape[-2:]) for v in rhs]
+                got = swap_sections(weight_half(place_send[:1], lhs, rhs))
+                halves[l].append(
+                    lax.psum(weight_half(place_keep[:1], lhs, rhs, got), "ctx")
                 )
-            )
-
-    g = [g_in[m] for m in range(mine)]
-    gin = {}
-    sums = {}
-    biases = {}
-    halves = {}
-    keep_half = section.astype(jnp.int32).reshape(1)
-    send_half = 1 - keep_half
-    for layer in reversed(layers):
-        gfull = [gather(g[m]) for m in range(mine)]
-        up, qkv_g, gx = [], [], []
-        rowsum, bq, bu = 0.0, 0.0, 0.0
-        for m in range(mine):
-            x_l, full, q, kvs, gelu, slope, attended, lse = kept[layer, m]
-            ga = spread_attn(sel[layer], gfull[m], *dw)
-            back_out = attend_back(q, kvs, ga, lse, drow[m], dcol[m], tables)
-            got = [shift_ctx(back_out[1 + j], -j) for j in range(1, blocks)]
-            u, usum = spread_up(sel[layer], gfull[m], *ow, slope)
-            p = join(back_out[0], back_out[1], got, tables)
-            partial, qsum = gather_grad(sel[layer], p, u, qw[0], fw[0], qw[1], fw[1])
-            gx_m, s = norm_back(x_l, scatter(partial), g[m], gain[layer])
-            up.append(u)
-            qkv_g.append(p)
-            gx.append(gx_m)
-            rowsum, bq, bu = rowsum + s, bq + qsum, bu + usum
-        sums[layer] = rowsum
-        biases[layer] = jnp.concatenate([bq.reshape(-1), bu.reshape(-1)])
-        fulls = [kept[layer, m][1] for m in range(mine)]
-        attn = [kept[layer, m][6] for m in range(mine)]
-        gelus = [kept[layer, m][4] for m in range(mine)]
-        gplane = [v[None] for v in gfull]
-        uplane = [v[None] for v in up]
-        jobs = ((attn, gplane), (gelus, gplane), (fulls, uplane), (fulls, qkv_g))
-        reduced = []
-        for lhs, rhs in jobs:
-            got = swap_sections(weight_half(send_half, lhs, rhs))
-            reduced.append(lax.psum(weight_half(keep_half, lhs, rhs, got), "ctx"))
-        halves[layer] = reduced
-        g = gx
-        gin[layer] = jnp.stack(gx)
 
     def to_owner(pair_of):
         moved = swap_sections(jnp.where(section == 0, pair_of[1], pair_of[0]))
@@ -720,18 +1111,32 @@
     grad_in = to_owner([gin[0], gin[1]])
 
     final = []
-    for k in range(4):
-        own = [halves[layer][k] for layer in layers]
-        got = [
-            lax.ppermute(own[layer], "section", [(1 - layer, layer)]) for layer in layers
-        ]
-        final.append(widen(keep_half, own, got))
-    dense_g, fc2_g, fc1_g, qkv_gr = final
-
-    rowsum = lax.psum(jnp.stack([sums[0], sums[1]]), ("section", "ctx", "tp"))
-    rowsum = jnp.where(section == 0, rowsum[0], rowsum[1])
-    bias_sum = lax.psum(jnp.stack([biases[0], biases[1]]), ("section", "ctx"))
-    bias_sum = jnp.where(section == 0, bias_sum[0], bias_sum[1])
+    if square:
+        order = class_order(at_x, at_y)
+        for k, parts in enumerate((out_parts(0), in_parts(0))):
+            final += widen_group(
+                parts, place_keep[:1], order, [halves[layer][k] for layer in layers]
+            )
+    else:
+        for k in range(4):
+            own = [halves[layer][k] for layer in layers]
+            got = [
+                lax.ppermute(own[layer], "section", [(1 - layer, layer)])
+                for layer in layers
+            ]
+            final.append(widen(place_keep[:1], own, got))
+    fc2_g, dense_g, fc1_g, qkv_gr = final
+    dense_g = dense_g.reshape(1, local, width)
+    fc2_g = fc2_g.reshape(1, hidden, width)
+    fc1_g = fc1_g.reshape(1, width, hidden)
+
+    flat = [jnp.concatenate([sums[l].reshape(-1), biases[l]]) for l in layers]
+    total = jnp.where(section == 0, flat[0], flat[1]) + swap_sections(
+        jnp.where(section == 0, flat[1], flat[0])
+    )
+    total = butterfly(total, "ctx")
+    rowsum = butterfly(total[: 3 * width], "tp").reshape(3, width)
+    bias_sum = total[3 * width :]
 
     return (
         layer_out[None],

time: 1380 us -> 1140 us (0.83)
  waiting for transfers between devices: 703 us -> 433 us
  starting transfers between devices: 73.9 us -> 151 us
  blocking collectives: 64.9 us -> 0 us
  other arithmetic: 17 us -> 62.6 us
  Pallas kernels: 470 us -> 431 us
  local copies, waits for them, and re-layouts: 22.8 us -> 37.6 us
    psum x1 -> x0, waiting for transfers between devices: 399 us -> none  [on_device(): reduced.append(lax.psum(weight_half(keep_half, lhs, rhs, got), 'ctx'))]
    ppermute x8 -> x40, waiting for transfers between devices: 0.02 us -> 261 us  [the longest x16 142 us: hop(): return lax.ppermute(x, 'ctx', [(i, i ^ axis_bit) for i in range(4)])]
    pallas_call x64 -> x44, Pallas kernels: 470 us -> 288 us  [call(): pl.pallas_call(kernel, grid_spec=pltpu.PrefetchScalarGridSpec(num_scalar_...]
    pallas_call x0 -> x18, Pallas kernels: none -> 143 us  [the longest x16 101 us: wide_part(): pl.pallas_call(body, grid_spec=pltpu.PrefetchScalarGridSpec(num_scalar_pr...]
    reduce_scatter x8, waiting for transfers between devices: 152 us -> 52.3 us  [scatter(): return lax.psum_scatter(v, 'tp', scatter_dimension=0, tiled=True)]
    ppermute x8 -> x40, starting transfers between devices: 28.1 us -> 99.6 us  [the longest x16 45.8 us: hop(): return lax.ppermute(x, 'ctx', [(i, i ^ axis_bit) for i in range(4)])]
    psum x2 -> x0, blocking collectives: 64.9 us -> none  [the longest x1 38.4 us: on_device(): rowsum = lax.psum(jnp.stack([sums[0], sums[1]]), ('section', 'ctx', 'tp'))]
    another operation x5 -> x19, other arithmetic: 1.26 us -> 35.9 us  [the longest x8 20.1 us: reduce_group(): full = jnp.stack([f, other] if layer == 0 else [other, f], axis=1)]
  transfers between devices with their start and end apart: 56 -> 84, of which waited for: 18 -> 27; matrix products, arithmetic and copies ran while one was open for 2% -> 8% of each run, Pallas kernels for 33% -> 30%
where the time goes in v2:
time: 1140 us; the launch traced here: 1130 us
  waiting for transfers between devices  433 us (38%)
  Pallas kernels  431 us (38%)
  starting transfers between devices  151 us (13%)
  other arithmetic  62.6 us (5%)
  local copies, waits for them, and re-layouts  37.6 us (3%)
  between operations  16 us (1%)
    pallas_call x44, Pallas kernels, call(): pl.pallas_call(kernel, grid_spec=pltpu.PrefetchScalarGridSpec(num_scalar_...  288 us
    ppermute x16, waiting for transfers between devices, hop(): return lax.ppermute(x, 'ctx', [(i, i ^ axis_bit) for i in range(4)])  142 us
    pallas_call x16, Pallas kernels, wide_part(): pl.pallas_call(body, grid_spec=pltpu.PrefetchScalarGridSpec(num_scalar_pr...  101 us
    all_gather x8, waiting for transfers between devices, gather(): return lax.all_gather(v, 'tp', axis=0, tiled=True)  81.3 us
    ppermute x4, waiting for transfers between devices, butterfly(): x = x + lax.ppermute(x, axis, [(i, i ^ bit) for i in range(length)])  80.1 us
    reduce_scatter x8, waiting for transfers between devices, scatter(): return lax.psum_scatter(v, 'tp', scatter_dimension=0, tiled=True)  52.3 us
    ppermute x16, starting transfers between devices, hop(): return lax.ppermute(x, 'ctx', [(i, i ^ axis_bit) for i in range(4)])  45.8 us
    ppermute x16, starting transfers between devices, hop_in(): return lax.ppermute(x, ('section', 'ctx'), pairs)  41.3 us
  transfers between devices with their start and end apart: 84, of which 27 were waited for; matrix products, arithmetic and copies ran while one was open for 8% of the time, Pallas kernels for 30%

profile of v2, /device:TPU:0, one launch (start us, length us, event | category | flops | bytes accessed | tf_op | source)
XLA Modules:
  0.0 1130.7 jit_solution(14514312948337719035)
XLA Ops:
  25.2 23.7 %all-gather.13.cloned.1.call-done.refs_1_ = bf16[256,2048]{1,0:T(8,128)(2,1)} async-done(((bf16[64,2048]{1,0:T(8,128)(2,1)}), bf16[256,2048]{1,0:T(8,128)(2,1)}) %all-gather.13.cloned.1.call-update) | async-done | bytes 1048592 | tf_op jit(solution)/shard_map/all_gather | solution.py:890
  48.9 8.0 project.4
  64.2 9.4 expand.4
  78.4 7.9 project.5
  94.2 8.8 contract.4
  111.0 9.5 expand.5
  120.5 7.6 collective-permute-done.8.refs_5_.refs_10_
  135.7 8.7 contract.5
  147.3 25.1 %reduce-scatter.11.cloned.1.call-done.branch = bf16[64,2048]{1,0:T(8,128)(2,1)} async-done(((bf16[256,2048]{1,0:T(8,128)(2,1)}), bf16[64,2048]{1,0:T(8,128)(2,1)}) %reduce-scatter.11.cloned.1.call-update) | async-done | bytes 262160 | tf_op jit(solution)/shard_map/reduce_scatter | solution.py:893
  175.2 25.9 %all-gather.17.cloned.1.call-done.refs_1_.refs_2_ = bf16[256,2048]{1,0:T(8,128)(2,1)} async-done(((bf16[64,2048]{1,0:T(8,128)(2,1)}), bf16[256,2048]{1,0:T(8,128)(2,1)}) %all-gather.17.cloned.1.call-update) | async-done | bytes 1048592 | tf_op jit(solution)/shard_map/all_gather | solution.py:890
  203.6 27.0 %all-gather.15.cloned.1.call-done.refs_1_ = bf16[256,2048]{1,0:T(8,128)(2,1)} async-done(((bf16[64,2048]{1,0:T(8,128)(2,1)}), bf16[256,2048]{1,0:T(8,128)(2,1)}) %all-gather.15.cloned.1.call-update) | async-done | bytes 1048592 | tf_op jit(solution)/shard_map/all_gather | solution.py:890
  230.5 7.3 project.6
  244.7 8.9 expand.6
  253.5 7.4 project.7
  264.9 11.4 %collective-permute-done.10.refs_5_.refs_10_ = bf16[2,256,512]{2,1,0:T(8,128)(2,1)S(1)} collective-permute-done((bf16[2,256,512]{2,1,0:T(8,128)(2,1)}, bf16[2,256,512]{2,1,0:T(8,128)(2,1)S(1)}, u32[]{:S(2)}, u32[]{:S(2)}) %collective-permute-start.10) | collective-permute-done | bytes 524320 | tf_op jit(solution)/shard_map/ppermute | solution.py:808
  283.9 8.8 expand.7
  315.8 9.7 attend_back.4
  325.5 7.7 wide_fc2.5
  346.7 9.7 attend_back.5
  358.1 12.7 %collective-permute-done.20 = bf16[2,5,128,512]{3,2,1,0:T(8,128)(2,1)} collective-permute-done((bf16[2,5,128,512]{3,2,1,0:T(8,128)(2,1)}, bf16[2,5,128,512]{3,2,1,0:T(8,128)(2,1)}, u32[]{:S(2)}, u32[]{:S(2)}) %collective-permute-start.20) | collective-permute-done | bytes 1310752 | tf_op jit(solution)/shard_map/ppermute | solution.py:682
  375.3 8.8 collective-permute-done.14.refs_2_
  384.1 8.3 spread_up.4
  395.4 8.3 spread_up.5
  425.0 10.8 gather_grad.4
  436.0 10.9 gather_grad.5
  454.7 7.9 wide_fc1.5
  473.6 25.6 %reduce-scatter.15.cloned.1.call-done.gn = bf16[64,2048]{1,0:T(8,128)(2,1)} async-done(((bf16[256,2048]{1,0:T(8,128)(2,1)}), bf16[64,2048]{1,0:T(8,128)(2,1)}) %reduce-scatter.15.cloned.1.call-update) | async-done | bytes 262160 | tf_op jit(solution)/shard_map/reduce_scatter | solution.py:893
  503.2 40.2 %collective-permute-done.25 = bf16[2,7,128,512]{3,2,1,0:T(8,128)(2,1)} collective-permute-done((bf16[2,7,128,512]{3,2,1,0:T(8,128)(2,1)}, bf16[2,7,128,512]{3,2,1,0:T(8,128)(2,1)}, u32[]{:S(2)}, u32[]{:S(2)}) %collective-permute-start.25) | collective-permute-done | bytes 1835040 | tf_op jit(solution)/shard_map/ppermute | solution.py:682
  549.3 9.7 attend_back.7
  574.4 38.1 %collective-permute-done.32 = bf16[2,7,128,512]{3,2,1,0:T(8,128)(2,1)} collective-permute-done((bf16[2,7,128,512]{3,2,1,0:T(8,128)(2,1)}, bf16[2,7,128,512]{3,2,1,0:T(8,128)(2,1)}, u32[]{:S(2)}, u32[]{:S(2)}) %collective-permute-start.32) | collective-permute-done | bytes 1835040 | tf_op jit(solution)/shard_map/ppermute | solution.py:682
  616.6 9.7 attend_back.6
  632.6 8.9 spread_up.6
  654.2 11.3 %gather_grad.6 = (bf16[256,2048]{1,0:T(8,128)(2,1)}, f32[3,512]{1,0:T(4,128)}) custom-call(s32[1]{0:T(128)} %bitcast.1.refs_0_, bf16[3,256,512]{2,1,0:T(8,128)(2,1)} %join.6.refs_1_.refs_3_, bf16[256,2048]{1,0:T(8,128)(2,1)} %get-tuple-element.279.refs_2_.refs_3_, bf16[3,2048,512]{2,1,0:T(8,128)(2,1)} %bitcast.275, bf16[2048,2048]{1,0:T(8,128)(2,1)} %bitcast.266, ...), custom_call_target="tpu_custom_call" | custom-call | flops 3758096384 | bytes 17569792 | tf_op jit(solution)/shard_map/gather_grad/pallas_call | solution.py:35
  671.5 7.7 wide_fc2.7
  683.8 8.8 spread_up.7
  726.8 21.8 %collective-permute-start.55 = (bf16[2,5,128,512]{3,2,1,0:T(8,128)(2,1)}, bf16[2,5,128,512]{3,2,1,0:T(8,128)(2,1)}, u32[]{:S(2)}, u32[]{:S(2)}) collective-permute-start(bf16[2,5,128,512]{3,2,1,0:T(8,128)(2,1)} %get-tuple-element.325), channel_id=1, source_target_pairs={{0,4},{4,0},{8,12},{12,8},{1,5},{5,1},{9,13},{13,9},{2,6},{6,2},{1... | collective-permute-start | bytes 3932168 | tf_op jit(solution)/shard_map/ppermute | solution.py:682
  748.7 7.7 wide_fc1.7
  769.3 11.4 %gather_grad.7 = (bf16[256,2048]{1,0:T(8,128)(2,1)}, f32[3,512]{1,0:T(4,128)}) custom-call(s32[1]{0:T(128)} %bitcast.1.refs_0_, bf16[3,256,512]{2,1,0:T(8,128)(2,1)} %join.7.refs_4_.refs_1_, bf16[256,2048]{1,0:T(8,128)(2,1)} %get-tuple-element.289.refs_4_.refs_2_, bf16[3,2048,512]{2,1,0:T(8,128)(2,1)} %bitcast.276, bf16[2048,2048]{1,0:T(8,128)(2,1)} %bitcast.267, ...), custom_call_target="tpu_custom_call" | custom-call | flops 3758096384 | bytes 17569792 | tf_op jit(solution)/shard_map/gather_grad/pallas_call | solution.py:35
  785.5 46.3 %collective-permute-done.58 = bf16[5,128,512]{2,1,0:T(8,128)(2,1)S(1)} collective-permute-done((bf16[5,128,512]{2,1,0:T(8,128)(2,1)}, bf16[5,128,512]{2,1,0:T(8,128)(2,1)S(1)}, u32[]{:S(2)}, u32[]{:S(2)}) %collective-permute-start.58) | collective-permute-done | bytes 655392 | tf_op jit(solution)/shard_map/ppermute | solution.py:682
  848.3 8.1 contract.6
  871.2 8.2 contract.7
  883.0 21.1 %collective-permute-done.46 = bf16[2,7,128,512]{3,2,1,0:T(8,128)(2,1)} collective-permute-done((bf16[2,7,128,512]{3,2,1,0:T(8,128)(2,1)}, bf16[2,7,128,512]{3,2,1,0:T(8,128)(2,1)}, u32[]{:S(2)}, u32[]{:S(2)}) %collective-permute-start.46) | collective-permute-done | bytes 1835040 | tf_op jit(solution)/shard_map/ppermute | solution.py:701
  923.3 13.9 %collective-permute-start.37 = (f32[9728]{0:T(1024)S(1)}, f32[9728]{0:T(1024)S(1)}, u32[]{:S(2)}, u32[]{:S(2)}) collective-permute-start(f32[9728]{0:T(1024)S(1)} %fusion.26), channel_id=1, source_target_pairs={{0,16},{16,0},{1,17},{17,1},{2,18},{18,2},{3,19},{19,3},{4,20},{20... | collective-permute-start | bytes 116744 | tf_op jit(solution)/shard_map/ppermute | solution.py:795
  948.5 44.6 %collective-permute-done.38 = f32[9728]{0:T(1024)S(1)} collective-permute-done((f32[9728]{0:T(1024)S(1)}, f32[9728]{0:T(1024)S(1)}, u32[]{:S(2)}, u32[]{:S(2)}) %collective-permute-start.38) | collective-permute-done | bytes 38944 | tf_op jit(solution)/shard_map/ppermute | solution.py:801
  997.6 32.9 %collective-permute-done.39 = f32[9728]{0:T(1024)S(1)} collective-permute-done((f32[9728]{0:T(1024)S(1)}, f32[9728]{0:T(1024)S(1)}, u32[]{:S(2)}, u32[]{:S(2)}) %collective-permute-start.39) | collective-permute-done | bytes 38944 | tf_op jit(solution)/shard_map/ppermute | solution.py:801
  1059.5 7.3 collective-permute-done.63
  1073.4 18.6 %widen_group.3 = (f32[2048,2048]{1,0:T(8,128)}, f32[512,2048]{1,0:T(8,128)}) custom-call(s32[1]{0:T(128)} %bitcast.22.refs_0_, s32[16]{0:T(128)} %stack.225.refs_1_, bf16[4,1,5,128,512]{4,3,2,1,0:T(8,128)(2,1)} %bitcast.120.refs_2_, bf16[4,1,5,128,512]{4,3,2,1,0:T(8,128)(2,1)} %bitcast.299, bf16[4,1,5,128,512]{4,3,2,1,0:T(8,128)(2,1)} %bitcast.124.refs_4_, ...), custom_call_target="tpu_custom_call" | custom-call | bytes 31457280 | tf_op jit(solution)/shard_map/widen_group/pallas_call | solution.py:767
  1101.0 22.7 %widen_group.2 = (f32[2048,2048]{1,0:T(8,128)}, f32[3,2048,512]{2,1,0:T(8,128)}) custom-call(s32[1]{0:T(128)} %bitcast.22.refs_0_, s32[16]{0:T(128)} %stack.225.refs_1_, bf16[4,1,7,128,512]{4,3,2,1,0:T(8,128)(2,1)} %bitcast.88.refs_2_, bf16[4,1,7,128,512]{4,3,2,1,0:T(8,128)(2,1)} %bitcast.90.refs_3_, bf16[4,1,7,128,512]{4,3,2,1,0:T(8,128)(2,1)} %bitcast.92.refs_4_, ...), custom_call_target="tpu_custom_call" | custom-call | bytes 44040192 | tf_op jit(solution)/shard_map/widen_group/pallas_call | solution.py:767
  (407 shorter events, 389.7 us)
Async XLA Ops:
  7.2 41.7 %all-gather.13.cloned.1.call-start = ((), (), s32[]{:S(2)}) async-start(), calls=%async_computation.9 | async-start | bytes 1310720 | tf_op jit(solution)/shard_map/all_gather | solution.py:890
  13.0 51.3 %collective-permute-start.2 = (bf16[2048,2048]{1,0:T(8,128)(2,1)}, bf16[2048,2048]{1,0:T(8,128)(2,1)}, u32[]{:S(2)}, u32[]{:S(2)}) collective-permute-start(bf16[2048,2048]{1,0:T(8,128)(2,1)} %bitcast.259), channel_id=1, source_target_pairs={{0,16},{16,0},{1,17},{17,1},{2,18},{18,2},{3,19},{19,3},{4,20},{20... | collective-permute-start | bytes 25165832 | tf_op jit(solution)/shard_map/ppermute | solution.py:795
  13.3 80.9 %collective-permute-start.6 = (bf16[2048,2048]{1,0:T(8,128)(2,1)}, bf16[2048,2048]{1,0:T(8,128)(2,1)}, u32[]{:S(2)}, u32[]{:S(2)}) collective-permute-start(bf16[2048,2048]{1,0:T(8,128)(2,1)} %bitcast.250), channel_id=1, source_target_pairs={{0,16},{16,0},{1,17},{17,1},{2,18},{18,2},{3,19},{19,3},{4,20},{20... | collective-permute-start | bytes 25165832 | tf_op jit(solution)/shard_map/ppermute | solution.py:795
  18.3 60.1 %all-gather.11.cloned.1.call-start = ((), (), s32[]{:S(2)}) async-start(), calls=%async_computation.8 | async-start | bytes 1310720 | tf_op jit(solution)/shard_map/all_gather | solution.py:890
  18.4 75.8 %collective-permute-start.5 = (bf16[512,2048]{1,0:T(8,128)(2,1)S(1)}, bf16[512,2048]{1,0:T(8,128)(2,1)}, u32[]{:S(2)}, u32[]{:S(2)}) collective-permute-start(bf16[512,2048]{1,0:T(8,128)(2,1)S(1)} %bitcast.285), channel_id=1, source_target_pairs={{0,16},{16,0},{1,17},{17,1},{2,18},{18,2},{3,19},{19,3},{4,20},{20... | collective-permute-start | bytes 6291464 | tf_op jit(solution)/shard_map/ppermute | solution.py:795
  20.6 124.6 %reduce-scatter.9.cloned.1.call-start = ((), (), s32[]{:S(2)}) async-start(), calls=%async_computation.10 | async-start | bytes 1310720 | tf_op jit(solution)/shard_map/reduce_scatter | solution.py:893
  103.0 69.4 %reduce-scatter.11.cloned.1.call-start = ((), (), s32[]{:S(2)}) async-start(), calls=%async_computation.11 | async-start | bytes 1310720 | tf_op jit(solution)/shard_map/reduce_scatter | solution.py:893
  144.5 56.6 %all-gather.17.cloned.1.call-start = ((), (), s32[]{:S(2)}) async-start(), calls=%async_computation.13 | async-start | bytes 1310720 | tf_op jit(solution)/shard_map/all_gather | solution.py:890
  174.5 56.0 %all-gather.15.cloned.1.call-start = ((), (), s32[]{:S(2)}) async-start(), calls=%async_computation.12 | async-start | bytes 1310720 | tf_op jit(solution)/shard_map/all_gather | solution.py:890
  175.1 126.2 %all-gather.23.cloned.1.call-start = ((), (), s32[]{:S(2)}) async-start(), calls=%async_computation.22 | async-start | bytes 1310720 | tf_op jit(solution)/shard_map/all_gather | solution.py:890
  202.0 99.3 %all-gather.25.cloned.1.call-start = ((), (), s32[]{:S(2)}) async-start(), calls=%async_computation.23 | async-start | bytes 1310720 | tf_op jit(solution)/shard_map/all_gather | solution.py:890
  202.7 268.5 %reduce-scatter.13.cloned.1.call-start = ((), (), s32[]{:S(2)}) async-start(), calls=%async_computation.14 | async-start | bytes 1310720 | tf_op jit(solution)/shard_map/reduce_scatter | solution.py:893
  340.9 43.2 %collective-permute-start.14 = (bf16[2,256,512]{2,1,0:T(8,128)(2,1)}, bf16[2,256,512]{2,1,0:T(8,128)(2,1)}, u32[]{:S(2)}, u32[]{:S(2)}) collective-permute-start(bf16[2,256,512]{2,1,0:T(8,128)(2,1)} %get-tuple-element.233), channel_id=1, source_target_pairs={{4,0},{8,4},{12,8},{5,1},{9,5},{13,9},{6,2},{10,6},{14,10},{7,3},{... | collective-permute-start | bytes 1572872 | tf_op jit(solution)/shard_map/ppermute | solution.py:808
  342.2 50.2 %collective-permute-start.15 = (bf16[2,256,512]{2,1,0:T(8,128)(2,1)}, bf16[2,256,512]{2,1,0:T(8,128)(2,1)}, u32[]{:S(2)}, u32[]{:S(2)}) collective-permute-start(bf16[2,256,512]{2,1,0:T(8,128)(2,1)} %get-tuple-element.234), channel_id=1, source_target_pairs={{8,0},{12,4},{9,1},{13,5},{10,2},{14,6},{11,3},{15,7},{24,16},{28,... | collective-permute-start | bytes 1572872 | tf_op jit(solution)/shard_map/ppermute | solution.py:808
  356.4 47.3 %collective-permute-start.17 = (bf16[2,256,512]{2,1,0:T(8,128)(2,1)}, bf16[2,256,512]{2,1,0:T(8,128)(2,1)}, u32[]{:S(2)}, u32[]{:S(2)}) collective-permute-start(bf16[2,256,512]{2,1,0:T(8,128)(2,1)} %get-tuple-element.241), channel_id=1, source_target_pairs={{4,0},{8,4},{12,8},{5,1},{9,5},{13,9},{6,2},{10,6},{14,10},{7,3},{... | collective-permute-start | bytes 1572872 | tf_op jit(solution)/shard_map/ppermute | solution.py:808
  435.9 63.3 %reduce-scatter.15.cloned.1.call-start = ((), (), s32[]{:S(2)}) async-start(), calls=%async_computation.15 | async-start | bytes 1310720 | tf_op jit(solution)/shard_map/reduce_scatter | solution.py:893
  446.9 99.2 %all-gather.21.cloned.1.call-start = ((), (), s32[]{:S(2)}) async-start(), calls=%async_computation.19 | async-start | bytes 1310720 | tf_op jit(solution)/shard_map/all_gather | solution.py:890
  501.6 57.4 %all-gather.19.cloned.1.call-start = ((), (), s32[]{:S(2)}) async-start(), calls=%async_computation.18 | async-start | bytes 1310720 | tf_op jit(solution)/shard_map/all_gather | solution.py:890
  501.6 41.7 %collective-permute-start.25 = (bf16[2,7,128,512]{3,2,1,0:T(8,128)(2,1)}, bf16[2,7,128,512]{3,2,1,0:T(8,128)(2,1)}, u32[]{:S(2)}, u32[]{:S(2)}) collective-permute-start(bf16[2,7,128,512]{3,2,1,0:T(8,128)(2,1)} %get-tuple-element.266), channel_id=1, source_target_pairs={{0,4},{4,0},{8,12},{12,8},{1,5},{5,1},{9,13},{13,9},{2,6},{6,2},{1... | collective-permute-start | bytes 5505032 | tf_op jit(solution)/shard_map/ppermute | solution.py:682
  503.2 410.9 %reduce-scatter.21.cloned.1.call-start = ((), (), s32[]{:S(2)}) async-start(), calls=%async_computation.20 | async-start | bytes 1310720 | tf_op jit(solution)/shard_map/reduce_scatter | solution.py:893
  569.7 101.7 %collective-permute-start.28 = (bf16[2,2,2,5,128,512]{5,4,3,2,1,0:T(8,128)(2,1)}, bf16[2,2,2,5,128,512]{5,4,3,2,1,0:T(8,128)(2,1)}, u32[]{:S(2)}, u32[]{:S(2)}) collective-permute-start(bf16[2,2,2,5,128,512]{5,4,3,2,1,0:T(8,128)(2,1)} %wide_dense.6), channel_id=1, source_target_pairs={{0,16},{16,0},{1,17},{17,1},{2,18},{18,2},{3,19},{19,3},{4,20},{20... | collective-permute-start | bytes 15728648 | tf_op jit(solution)/shard_map/ppermute | solution.py:795
  569.7 42.7 %collective-permute-start.32 = (bf16[2,7,128,512]{3,2,1,0:T(8,128)(2,1)}, bf16[2,7,128,512]{3,2,1,0:T(8,128)(2,1)}, u32[]{:S(2)}, u32[]{:S(2)}) collective-permute-start(bf16[2,7,128,512]{3,2,1,0:T(8,128)(2,1)} %get-tuple-element.295), channel_id=1, source_target_pairs={{0,8},{4,12},{8,0},{12,4},{1,9},{5,13},{9,1},{13,5},{2,10},{6,14},... | collective-permute-start | bytes 5505032 | tf_op jit(solution)/shard_map/ppermute | solution.py:682
  615.2 50.3 %collective-permute-start.33 = (bf16[7,128,512]{2,1,0:T(8,128)(2,1)}, bf16[7,128,512]{2,1,0:T(8,128)(2,1)S(1)}, u32[]{:S(2)}, u32[]{:S(2)}) collective-permute-start(bf16[7,128,512]{2,1,0:T(8,128)(2,1)} %fusion.9), channel_id=1, source_target_pairs={{0,4},{4,0},{8,12},{12,8},{1,5},{5,1},{9,13},{13,9},{2,6},{6,2},{1... | collective-permute-start | bytes 2752520 | tf_op jit(solution)/shard_map/ppermute | solution.py:682
  648.5 50.7 %collective-permute-start.29 = (bf16[2,256,512]{2,1,0:T(8,128)(2,1)}, bf16[2,256,512]{2,1,0:T(8,128)(2,1)}, u32[]{:S(2)}, u32[]{:S(2)}) collective-permute-start(bf16[2,256,512]{2,1,0:T(8,128)(2,1)} %get-tuple-element.292), channel_id=1, source_target_pairs={{4,0},{8,4},{12,8},{5,1},{9,5},{13,9},{6,2},{10,6},{14,10},{7,3},{... | collective-permute-start | bytes 1572872 | tf_op jit(solution)/shard_map/ppermute | solution.py:808
  649.8 49.4 %collective-permute-start.30 = (bf16[2,256,512]{2,1,0:T(8,128)(2,1)}, bf16[2,256,512]{2,1,0:T(8,128)(2,1)}, u32[]{:S(2)}, u32[]{:S(2)}) collective-permute-start(bf16[2,256,512]{2,1,0:T(8,128)(2,1)} %get-tuple-element.293), channel_id=1, source_target_pairs={{8,0},{12,4},{9,1},{13,5},{10,2},{14,6},{11,3},{15,7},{24,16},{28,... | collective-permute-start | bytes 1572872 | tf_op jit(solution)/shard_map/ppermute | solution.py:808
  712.1 204.4 %reduce-scatter.23.cloned.1.call-start = ((), (), s32[]{:S(2)}) async-start(), calls=%async_computation.21 | async-start | bytes 1310720 | tf_op jit(solution)/shard_map/reduce_scatter | solution.py:893
  712.3 52.6 %collective-permute-start.57 = (bf16[2,5,128,512]{3,2,1,0:T(8,128)(2,1)}, bf16[2,5,128,512]{3,2,1,0:T(8,128)(2,1)}, u32[]{:S(2)}, u32[]{:S(2)}) collective-permute-start(bf16[2,5,128,512]{3,2,1,0:T(8,128)(2,1)} %get-tuple-element.327), channel_id=1, source_target_pairs={{0,8},{4,12},{8,0},{12,4},{1,9},{5,13},{9,1},{13,5},{2,10},{6,14},... | collective-permute-start | bytes 3932168 | tf_op jit(solution)/shard_map/ppermute | solution.py:682
  726.8 56.7 %collective-permute-start.55 = (bf16[2,5,128,512]{3,2,1,0:T(8,128)(2,1)}, bf16[2,5,128,512]{3,2,1,0:T(8,128)(2,1)}, u32[]{:S(2)}, u32[]{:S(2)}) collective-permute-start(bf16[2,5,128,512]{3,2,1,0:T(8,128)(2,1)} %get-tuple-element.325), channel_id=1, source_target_pairs={{0,4},{4,0},{8,12},{12,8},{1,5},{5,1},{9,13},{13,9},{2,6},{6,2},{1... | collective-permute-start | bytes 3932168 | tf_op jit(solution)/shard_map/ppermute | solution.py:682
  763.5 69.9 %collective-permute-start.44 = (bf16[2,7,128,512]{3,2,1,0:T(8,128)(2,1)}, bf16[2,7,128,512]{3,2,1,0:T(8,128)(2,1)}, u32[]{:S(2)}, u32[]{:S(2)}) collective-permute-start(bf16[2,7,128,512]{3,2,1,0:T(8,128)(2,1)} %get-tuple-element.323), channel_id=1, source_target_pairs={{0,8},{4,12},{8,0},{12,4},{1,9},{5,13},{9,1},{13,5},{2,10},{6,14},... | collective-permute-start | bytes 5505032 | tf_op jit(solution)/shard_map/ppermute | solution.py:682
  765.0 73.0 %collective-permute-start.42 = (bf16[2,7,128,512]{3,2,1,0:T(8,128)(2,1)}, bf16[2,7,128,512]{3,2,1,0:T(8,128)(2,1)}, u32[]{:S(2)}, u32[]{:S(2)}) collective-permute-start(bf16[2,7,128,512]{3,2,1,0:T(8,128)(2,1)} %get-tuple-element.321), channel_id=1, source_target_pairs={{0,4},{4,0},{8,12},{12,8},{1,5},{5,1},{9,13},{13,9},{2,6},{6,2},{1... | collective-permute-start | bytes 5505032 | tf_op jit(solution)/shard_map/ppermute | solution.py:682
  767.3 64.6 %collective-permute-start.58 = (bf16[5,128,512]{2,1,0:T(8,128)(2,1)}, bf16[5,128,512]{2,1,0:T(8,128)(2,1)S(1)}, u32[]{:S(2)}, u32[]{:S(2)}) collective-permute-start(bf16[5,128,512]{2,1,0:T(8,128)(2,1)} %fusion.19), channel_id=1, source_target_pairs={{0,4},{4,0},{8,12},{12,8},{1,5},{5,1},{9,13},{13,9},{2,6},{6,2},{1... | collective-permute-start | bytes 1966088 | tf_op jit(solution)/shard_map/ppermute | solution.py:682
  780.7 166.6 %reduce-scatter.17.cloned.1.call-start = ((), (), s32[]{:S(2)}) async-start(), calls=%async_computation.16 | async-start | bytes 1310720 | tf_op jit(solution)/shard_map/reduce_scatter | solution.py:893
  780.8 142.5 %collective-permute-start.51 = (bf16[2,2,7,128,512]{4,3,2,1,0:T(8,128)(2,1)}, bf16[2,2,7,128,512]{4,3,2,1,0:T(8,128)(2,1)}, u32[]{:S(2)}, u32[]{:S(2)}) collective-permute-start(bf16[2,2,7,128,512]{4,3,2,1,0:T(8,128)(2,1)} %pad_maximum_fusion), channel_id=1, source_target_pairs={{16,20},{20,16},{24,28},{28,24},{17,21},{21,17},{25,29},{29,25},{1... | collective-permute-start | bytes 11010056 | tf_op jit(solution)/shard_map/ppermute | solution.py:687
  785.0 56.9 %collective-permute-start.56 = (bf16[5,128,512]{2,1,0:T(8,128)(2,1)S(1)}, bf16[5,128,512]{2,1,0:T(8,128)(2,1)S(1)}, u32[]{:S(2)}, u32[]{:S(2)}) collective-permute-start(bf16[5,128,512]{2,1,0:T(8,128)(2,1)S(1)} %fusion.18), channel_id=1, source_target_pairs={{0,8},{4,12},{8,0},{12,4},{1,9},{5,13},{9,1},{13,5},{2,10},{6,14},... | collective-permute-start | bytes 1966088 | tf_op jit(solution)/shard_map/ppermute | solution.py:682
  846.2 64.3 %collective-permute-start.64 = (bf16[2,2,5,128,512]{4,3,2,1,0:T(8,128)(2,1)S(1)}, bf16[2,2,5,128,512]{4,3,2,1,0:T(8,128)(2,1)}, u32[]{:S(2)}, u32[]{:S(2)}) collective-permute-start(bf16[2,2,5,128,512]{4,3,2,1,0:T(8,128)(2,1)S(1)} %pad_maximum_fusion.2), channel_id=1, source_target_pairs={{16,20},{20,16},{24,28},{28,24},{17,21},{21,17},{25,29},{29,25},{1... | collective-permute-start | bytes 7864328 | tf_op jit(solution)/shard_map/ppermute | solution.py:687
  856.4 90.9 %reduce-scatter.19.cloned.1.call-start = ((), (), s32[]{:S(2)}) async-start(), calls=%async_computation.17 | async-start | bytes 1310720 | tf_op jit(solution)/shard_map/reduce_scatter | solution.py:893
  859.4 60.3 %collective-permute-start.65 = (bf16[2,2,5,128,512]{4,3,2,1,0:T(8,128)(2,1)S(1)}, bf16[2,2,5,128,512]{4,3,2,1,0:T(8,128)(2,1)}, u32[]{:S(2)}, u32[]{:S(2)}) collective-permute-start(bf16[2,2,5,128,512]{4,3,2,1,0:T(8,128)(2,1)S(1)} %pad_maximum_fusion.2), channel_id=1, source_target_pairs={{16,24},{20,28},{24,16},{28,20},{17,25},{21,29},{25,17},{29,21},{1... | collective-permute-start | bytes 7864328 | tf_op jit(solution)/shard_map/ppermute | solution.py:687
  868.7 78.2 %collective-permute-start.52 = (bf16[2,2,7,128,512]{4,3,2,1,0:T(8,128)(2,1)}, bf16[2,2,7,128,512]{4,3,2,1,0:T(8,128)(2,1)}, u32[]{:S(2)}, u32[]{:S(2)}) collective-permute-start(bf16[2,2,7,128,512]{4,3,2,1,0:T(8,128)(2,1)} %pad_maximum_fusion), channel_id=1, source_target_pairs={{16,24},{20,28},{24,16},{28,20},{17,25},{21,29},{25,17},{29,21},{1... | collective-permute-start | bytes 11010056 | tf_op jit(solution)/shard_map/ppermute | solution.py:687
  904.1 90.7 %collective-permute-start.61 = (bf16[2,2,5,128,512]{4,3,2,1,0:T(8,128)(2,1)}, bf16[2,2,5,128,512]{4,3,2,1,0:T(8,128)(2,1)}, u32[]{:S(2)}, u32[]{:S(2)}) collective-permute-start(bf16[2,2,5,128,512]{4,3,2,1,0:T(8,128)(2,1)} %pad_maximum_fusion.3), channel_id=1, source_target_pairs={{0,8},{4,12},{8,0},{12,4},{1,9},{5,13},{9,1},{13,5},{2,10},{6,14},... | collective-permute-start | bytes 7864328 | tf_op jit(solution)/shard_map/ppermute | solution.py:687
  910.4 131.1 %collective-permute-start.48 = (bf16[2,2,7,128,512]{4,3,2,1,0:T(8,128)(2,1)}, bf16[2,2,7,128,512]{4,3,2,1,0:T(8,128)(2,1)}, u32[]{:S(2)}, u32[]{:S(2)}) collective-permute-start(bf16[2,2,7,128,512]{4,3,2,1,0:T(8,128)(2,1)} %pad_maximum_fusion.1), channel_id=1, source_target_pairs={{0,8},{4,12},{8,0},{12,4},{1,9},{5,13},{9,1},{13,5},{2,10},{6,14},... | collective-permute-start | bytes 11010056 | tf_op jit(solution)/shard_map/ppermute | solution.py:687
  919.6 77.2 %collective-permute-start.60 = (bf16[2,2,5,128,512]{4,3,2,1,0:T(8,128)(2,1)}, bf16[2,2,5,128,512]{4,3,2,1,0:T(8,128)(2,1)S(1)}, u32[]{:S(2)}, u32[]{:S(2)}) collective-permute-start(bf16[2,2,5,128,512]{4,3,2,1,0:T(8,128)(2,1)} %pad_maximum_fusion.3), channel_id=1, source_target_pairs={{0,4},{4,0},{8,12},{12,8},{1,5},{5,1},{9,13},{13,9},{2,6},{6,2},{1... | collective-permute-start | bytes 7864328 | tf_op jit(solution)/shard_map/ppermute | solution.py:687
  938.1 110.8 %collective-permute-start.47 = (bf16[2,2,7,128,512]{4,3,2,1,0:T(8,128)(2,1)}, bf16[2,2,7,128,512]{4,3,2,1,0:T(8,128)(2,1)}, u32[]{:S(2)}, u32[]{:S(2)}) collective-permute-start(bf16[2,2,7,128,512]{4,3,2,1,0:T(8,128)(2,1)} %pad_maximum_fusion.1), channel_id=1, source_target_pairs={{0,4},{4,0},{8,12},{12,8},{1,5},{5,1},{9,13},{13,9},{2,6},{6,2},{1... | collective-permute-start | bytes 11010056 | tf_op jit(solution)/shard_map/ppermute | solution.py:687
  947.0 46.2 %collective-permute-start.38 = (f32[9728]{0:T(1024)S(1)}, f32[9728]{0:T(1024)S(1)}, u32[]{:S(2)}, u32[]{:S(2)}) collective-permute-start(f32[9728]{0:T(1024)S(1)} %select_add_fusion), channel_id=1, source_target_pairs={{0,4},{4,0},{8,12},{12,8},{1,5},{5,1},{9,13},{13,9},{2,6},{6,2},{1... | collective-permute-start | bytes 116744 | tf_op jit(solution)/shard_map/ppermute | solution.py:801
  993.2 48.3 %collective-permute-start.66 = (bf16[2,5,128,512]{3,2,1,0:T(8,128)(2,1)}, bf16[2,5,128,512]{3,2,1,0:T(8,128)(2,1)S(1)}, u32[]{:S(2)}, u32[]{:S(2)}) collective-permute-start(bf16[2,5,128,512]{3,2,1,0:T(8,128)(2,1)} %slice_bitcast_fusion.5), channel_id=1, source_target_pairs={{16,20},{20,16},{24,28},{28,24},{17,21},{21,17},{25,29},{29,25},{1... | collective-permute-start | bytes 3932168 | tf_op jit(solution)/shard_map/ppermute | solution.py:687
  996.9 55.1 %collective-permute-start.67 = (bf16[2,5,128,512]{3,2,1,0:T(8,128)(2,1)S(1)}, bf16[2,5,128,512]{3,2,1,0:T(8,128)(2,1)S(1)}, u32[]{:S(2)}, u32[]{:S(2)}) collective-permute-start(bf16[2,5,128,512]{3,2,1,0:T(8,128)(2,1)S(1)} %copy-done.19), channel_id=1, source_target_pairs={{16,24},{20,28},{24,16},{28,20},{17,25},{21,29},{25,17},{29,21},{1... | collective-permute-start | bytes 3932168 | tf_op jit(solution)/shard_map/ppermute | solution.py:687
  1051.9 44.2 %collective-permute-start.53 = (bf16[2,7,128,512]{3,2,1,0:T(8,128)(2,1)}, bf16[2,7,128,512]{3,2,1,0:T(8,128)(2,1)S(1)}, u32[]{:S(2)}, u32[]{:S(2)}) collective-permute-start(bf16[2,7,128,512]{3,2,1,0:T(8,128)(2,1)} %slice_bitcast_fusion.1), channel_id=1, source_target_pairs={{16,20},{20,16},{24,28},{28,24},{17,21},{21,17},{25,29},{29,25},{1... | collective-permute-start | bytes 5505032 | tf_op jit(solution)/shard_map/ppermute | solution.py:687
  1052.9 43.3 %collective-permute-start.54 = (bf16[2,7,128,512]{3,2,1,0:T(8,128)(2,1)}, bf16[2,7,128,512]{3,2,1,0:T(8,128)(2,1)}, u32[]{:S(2)}, u32[]{:S(2)}) collective-permute-start(bf16[2,7,128,512]{3,2,1,0:T(8,128)(2,1)} %slice_bitcast_fusion), channel_id=1, source_target_pairs={{16,24},{20,28},{24,16},{28,20},{17,25},{21,29},{25,17},{29,21},{1... | collective-permute-start | bytes 5505032 | tf_op jit(solution)/shard_map/ppermute | solution.py:687
  1056.7 44.3 %collective-permute-start.50 = (bf16[2,7,128,512]{3,2,1,0:T(8,128)(2,1)}, bf16[2,7,128,512]{3,2,1,0:T(8,128)(2,1)}, u32[]{:S(2)}, u32[]{:S(2)}) collective-permute-start(bf16[2,7,128,512]{3,2,1,0:T(8,128)(2,1)} %slice_bitcast_fusion.2), channel_id=1, source_target_pairs={{0,8},{4,12},{8,0},{12,4},{1,9},{5,13},{9,1},{13,5},{2,10},{6,14},... | collective-permute-start | bytes 5505032 | tf_op jit(solution)/shard_map/ppermute | solution.py:687
  (85 other events, 1850.9 us)
Sparse Core Ops, SparseCore 0:
  18.4 30.4 all-gather.12
  51.0 27.3 all-gather.10
  103.2 26.6 reduce-scatter.8
  144.6 27.7 reduce-scatter.10
  174.6 26.4 all-gather.16
  203.1 27.3 all-gather.14
  232.1 27.3 all-gather.22
  261.6 27.3 all-gather.24
  436.0 35.1 reduce-scatter.12
  473.3 25.7 reduce-scatter.14
  501.7 26.4 all-gather.20
  529.6 27.3 all-gather.18
  712.2 46.4 reduce-scatter.20
  780.8 24.2 reduce-scatter.22
  856.6 27.6 reduce-scatter.16
  887.0 51.8 reduce-scatter.18
